TPU v7x, 32 devices: a whole 2x2x4 slice. The times are simulated.
32 devices in a mesh: expert: 16 (over z, y, core), half: 2 (over x).
Axes of the slice: x: 2, y: 2, z: 4, core: 2. Of those that a mesh axis runs over, the one named last changes fastest.
Arguments:
- tokens: bfloat16 [256, 2048], P('expert', 'half'), may hold values from -6 to 6
- upstream: bfloat16 [256, 2048], P('expert', 'half'), may hold values from -6 to 6
- expert_ids: int32 [256, 8], P('expert'), may hold values from 0 to 15, all different within a row; in each aligned block of 16 rows (0 to 15, 16 to 31, ...) at most 16 rows name the same one
- gate_probs: float32 [256, 8], P('expert'), may hold values from 0.01 to 1
- pad_mask: int32 [256], P('expert'), may hold values 0 or 1
- gate_weight: bfloat16 [16, 2048, 1536], P('expert', None, 'half'), may hold values from -0.125 to 0.125
- up_weight: bfloat16 [16, 2048, 1536], P('expert', None, 'half'), may hold values from -0.125 to 0.125
- down_weight: bfloat16 [16, 1536, 2048], P('expert', 'half'), may hold values from -0.15625 to 0.15625
Outputs:
- layer_out: bfloat16 [256, 2048], P('expert', 'half')
- grad_tokens: bfloat16 [256, 2048], P('expert', 'half')
Inputs may be any that keep to these rules, and one draw needn't show every extreme that they name: `expert_ids`: each row names 8 different experts. In the rows of one device (aligned blocks of 16 rows) no expert is named more than 16 times, a bound that some block reaches.
All inputs are finite; a program needn't handle non-finite values. No bound on the sum of `pad_mask` on one device may be relied on, other than what follows from the above.
Results may differ from a plain program's by a relative error of at most 0.025.
Values may be sent and summed in bfloat16 or wider, within the bound.
A program may use at most 64 MiB of HBM per device.

v0:
```python
import functools
import math

import jax
import jax.numpy as jnp
from jax import lax
from jax.experimental import pallas as pl
from jax.experimental.pallas import tpu as pltpu
from jax.sharding import PartitionSpec as P

orth_weight = 0.25


def assign_slots(expert_ids, experts, capacity):
    tok_count, top_count = expert_ids.shape
    flat_ids = expert_ids.reshape(tok_count * top_count)
    onehot = (flat_ids[:, None] == jnp.arange(experts, dtype=jnp.int32)[None, :]).astype(jnp.int32)
    before = jnp.cumsum(onehot, axis=0) - onehot
    slot_index = jnp.sum(before * onehot, axis=1)
    return flat_ids * capacity + slot_index


def placement_matrix(slot_dest, slots_total):
    row_index = jnp.arange(slots_total, dtype=jnp.int32)
    return (row_index[:, None] == slot_dest[None, :]).astype(jnp.bfloat16)


def to_experts(place, items):
    whole = lax.all_gather(items, "half", axis=1, tiled=True)
    buckets = jnp.dot(place, whole, preferred_element_type=jnp.float32).astype(jnp.bfloat16)
    return lax.all_to_all(buckets, "expert", split_axis=0, concat_axis=0, tiled=True)


def to_homes(partial_value):
    summed = lax.psum_scatter(
        partial_value.astype(jnp.bfloat16), "half", scatter_dimension=1, tiled=True
    )
    return lax.all_to_all(summed, "expert", split_axis=0, concat_axis=0, tiled=True)


def block_of(width):
    return next((b for b in (256, 128) if width % b == 0), width)


def tiles(width, body):
    size = block_of(width)

    def step(j, carry):
        body(pl.ds(pl.multiple_of(j * size, size), size), size)
        return carry

    lax.fori_loop(0, width // size, step, 0)


def dot(a, b):
    return jnp.dot(a, b, preferred_element_type=jnp.float32)


def dot_t(a, b):
    return lax.dot_general(a, b, (((1,), (1,)), ((), ())), preferred_element_type=jnp.float32)


def copy_kernel(a_ref, b_ref, a_out, b_out):
    a_out[...] = a_ref[...]
    b_out[...] = b_ref[...]


def fused_kernel(
    n, halves,
    tok_hbm, up_hbm, ids_hbm, probs_hbm, pad_hbm, wg_hbm, wu_hbm, wd_hbm,
    layer_ref, gtok_ref,
    up_ref, ids_ref, probs_ref, pad_ref,
    tok_buf, wg, wu, wd, gate_v, up_v, act_v, hid, gg, gu,
    osend, orecv, ored, xrecv, xs, gram_s, whole_s, gsend, grows, psend, prec, fsend, frecv, rsend, fin,
    w_sem, tok_ss, tok_rs, part_ss, part_rs, out_ss, out_rs, gram_ss, gram_rs,
    grad_ss, grad_rs, relay_ss, pair_ss, pair_rs, fpart_ss, fpart_rs, fin_ss, fin_rs,
):
    e = lax.axis_index("expert")
    h = lax.axis_index("half")
    tok, width = up_ref.shape
    hidden = wg.shape[1]
    rows = n * tok
    chips = n // 2
    group = min(n, 8)
    parity = lax.rem(e, 2)
    chip = lax.div(e, 2)
    sibling = e + 1 - 2 * parity
    full = halves * width

    def remote(src, dst, ssem, rsem, pe, ph):
        return pltpu.make_async_remote_copy(
            src_ref=src, dst_ref=dst, send_sem=ssem, recv_sem=rsem,
            device_id=(pe, ph), device_id_type=pl.DeviceIdType.MESH,
        )

    def wrap(a, d, size):
        return lax.rem(a + d, size)

    def flip(a, d):
        bit = 1
        out = a
        while bit <= d:
            if d & bit:
                out = out + bit * (1 - 2 * lax.rem(lax.div(a, bit), 2))
            bit *= 2
        return out

    def arrived(slot, rsem):
        remote(slot, slot, pair_ss.at[0], rsem, sibling, h).wait_recv()

    sends = []

    def send(*args):
        c = remote(*args)
        c.start()
        sends.append(c)

    moves = (
        (tok_hbm, tok_buf.at[h, e]), (ids_hbm, ids_ref), (probs_hbm, probs_ref),
        (pad_hbm, pad_ref), (up_hbm, up_ref),
        (wg_hbm.at[0], wg), (wu_hbm.at[0], wu), (wd_hbm.at[0], wd),
    )
    loads = [pltpu.make_async_copy(src, dst, w_sem.at[i]) for i, (src, dst) in enumerate(moves)]
    for c in loads:
        c.start()

    others = list(range(1, halves))
    near = list(range(1, n))
    outer = near[::-1]
    chips_near = list(range(1, chips))
    chips_far = chips_near[::-1]

    barrier = pltpu.get_barrier_semaphore()
    for d in outer:
        pl.semaphore_signal(
            barrier, inc=1, device_id=(flip(e, d), h), device_id_type=pl.DeviceIdType.MESH
        )
    for d in others:
        pl.semaphore_signal(
            barrier, inc=1, device_id=(e, wrap(h, d, halves)), device_id_type=pl.DeviceIdType.MESH
        )
    pl.semaphore_wait(barrier, len(outer) + len(others))

    loads[0].wait()
    k = 0
    mine = tok_buf.at[h, e]
    for d in chips_far:
        send(mine, mine, tok_ss.at[k], tok_rs.at[h, e], 2 * flip(chip, d) + parity, h)
        k += 1
    for d in others:
        send(mine, mine, tok_ss.at[k], tok_rs.at[h, e], e, wrap(h, d, halves))
        k += 1
    send(mine, mine, tok_ss.at[k], tok_rs.at[h, e], sibling, h)
    k += 1
    for d in chips_near:
        pe = 2 * flip(chip, d) + parity
        slot = tok_buf.at[h, pe]
        arrived(slot, tok_rs.at[h, pe])
        for dh in others:
            send(slot, slot, tok_ss.at[k], tok_rs.at[h, pe], e, wrap(h, dh, halves))
            k += 1
        send(slot, slot, tok_ss.at[k], tok_rs.at[h, pe], sibling, h)
        k += 1
    for d in [0] + chips_near:
        pe = 2 * flip(chip, d) + parity
        for dh in others:
            ph = wrap(h, halves - dh, halves)
            slot = tok_buf.at[ph, pe]
            arrived(slot, tok_rs.at[ph, pe])
            send(slot, slot, tok_ss.at[k], tok_rs.at[ph, pe], sibling, h)
            k += 1
    for c in loads[1:7]:
        c.wait()
    for dh in [0] + others:
        ph = wrap(h, halves - dh, halves)
        for d in [0] + chips_near:
            pe = 2 * flip(chip, d) + 1 - parity
            arrived(tok_buf.at[ph, pe], tok_rs.at[ph, pe])

        def hidden_step(cols, size, ph=ph, dh=dh):
            at = pl.ds(pl.multiple_of(ph * width, width), width)
            x = tok_buf[ph].reshape(rows, width)
            gate = dot(x, wg[at, cols])
            up = dot(x, wu[at, cols])
            if dh:
                gate = gate + gate_v[:, cols]
                up = up + up_v[:, cols]
            gate_v[:, cols] = gate
            up_v[:, cols] = up
            if dh == halves - 1:
                hid[:, cols] = (gate / (1.0 + jnp.exp(-gate)) * up).astype(jnp.bfloat16)

        tiles(hidden, hidden_step)
    loads[7].wait()

    for dh in others + [0]:
        ph = wrap(h, dh, halves)

        def down_step(cols, size, ph=ph, dh=dh):
            at = pl.ds(pl.multiple_of(cols.start + ph * width, size), size)
            part = dot(hid[...], wd[:, at])
            osend[dh, :, :, cols] = part.reshape(n, tok, size).astype(jnp.bfloat16)

        tiles(width, down_step)
        if dh:
            for j, d in enumerate(outer + [0]):
                pe = flip(e, d)
                send(
                    osend.at[dh, pe], orecv.at[halves - dh, pe],
                    part_ss.at[dh, j], part_rs.at[halves - dh, j], e, ph,
                )

    eye = (
        lax.broadcasted_iota(jnp.int32, (tok, tok), 0)
        == lax.broadcasted_iota(jnp.int32, (tok, tok), 1)
    )
    top = ids_ref.shape[0]
    lane = lax.broadcasted_iota(jnp.int32, (tok, top), 1)

    def column(row):
        return jnp.sum(jnp.where(eye, jnp.broadcast_to(row, (tok, tok)), 0.0), axis=1, keepdims=True)

    ids = jnp.zeros((tok, top), jnp.float32)
    probs = jnp.zeros((tok, top), jnp.float32)
    for j in range(top):
        ids = jnp.where(lane == j, column(ids_ref[j:j + 1, :].astype(jnp.float32)), ids)
        probs = jnp.where(lane == j, column(probs_ref[j:j + 1, :]), probs)
    pad = column(pad_ref[...].astype(jnp.float32))
    shares = probs / jnp.sum(probs, axis=1, keepdims=True)
    for j, d in enumerate(outer + [0]):
        pe = flip(e, d)
        total = osend[0, pe].astype(jnp.float32)
        for dh in others:
            arrived(orecv.at[dh, pe], part_rs.at[dh, j])
            total = total + orecv[dh, pe].astype(jnp.float32)
        if d:
            ored[pe] = total.astype(jnp.bfloat16)
            send(ored.at[pe], xrecv.at[e], out_ss.at[j], out_rs.at[e], pe, h)
        else:
            xrecv[e] = total.astype(jnp.bfloat16)
    def share_of(i):
        listed = (ids == i.astype(jnp.float32)).astype(jnp.float32)
        return jnp.sum(listed * shares, axis=1, keepdims=True), jnp.sum(listed, axis=1, keepdims=True)

    layer = jnp.zeros((tok, width), jnp.float32)
    for d in [0] + near:
        pe = flip(e, d)
        share, listed = share_of(pe)
        if d:
            arrived(xrecv.at[pe], out_rs.at[pe])
        value = jnp.where(listed > 0.0, xrecv[pe].astype(jnp.float32), 0.0)
        xs[pe] = value.astype(jnp.bfloat16)
        layer = layer + share * value

    x_all = xs[...].reshape(rows, width)
    same = (
        lax.rem(lax.broadcasted_iota(jnp.int32, (tok, rows), 1), tok)
        == lax.broadcasted_iota(jnp.int32, (tok, rows), 0)
    ).astype(jnp.float32)
    gram = dot_t(x_all, x_all).reshape(n, tok, rows) * same[None]
    gram_s[h] = jnp.sum(gram, axis=1)
    for dh in range(1, halves):
        send(gram_s.at[h], gram_s.at[h], gram_ss.at[dh], gram_rs.at[h], e, wrap(h, dh, halves))
    for dh in range(1, halves):
        ph = wrap(h, halves - dh, halves)
        arrived(gram_s.at[ph], gram_rs.at[ph])
    whole = gram_s[0]
    for i in range(1, halves):
        whole = whole + gram_s[i]
    apart = (
        lax.div(lax.broadcasted_iota(jnp.int32, (n, rows), 1), tok)
        != lax.broadcasted_iota(jnp.int32, (n, rows), 0)
    ).astype(jnp.float32)
    whole = whole * (apart * (orth_weight / math.sqrt(full)))
    whole_s[...] = whole
    x_all = xs[...].reshape(rows, width)
    upstream = up_ref[...].astype(jnp.float32)
    for g in range(n // group):
        first = pl.multiple_of(flip(lax.div(e, group), g) * group, group)
        coeffs = whole_s[pl.ds(first, group), :][:, None, :] * same[None]
        coeffs = coeffs.reshape(group * tok, rows)
        high = coeffs.astype(jnp.bfloat16)
        low = (coeffs - high.astype(jnp.float32)).astype(jnp.bfloat16)
        mixed = (dot(high, x_all) + dot(low, x_all)).reshape(group, tok, width)
        for i in range(group):
            share, _ = share_of(first + i)
            gsend[first + i] = (pad * (share * upstream + mixed[i])).astype(jnp.bfloat16)
        for d in range(max(1, g * group), (g + 1) * group):
            pe = flip(e, d)
            send(gsend.at[pe], grows.at[h, e], grad_ss.at[d], grad_rs.at[h, e], pe, h)
        if g == 0:
            for dh in others:
                send(
                    gsend.at[e], grows.at[h, e], relay_ss.at[dh - 1], grad_rs.at[h, e],
                    e, wrap(h, dh, halves),
                )
    layer_ref[...] = layer.astype(jnp.bfloat16)
    k = len(others)
    grows[h, e] = gsend[e]
    for d in near:
        pe = flip(e, d)
        slot = grows.at[h, pe]
        arrived(slot, grad_rs.at[h, pe])
        for dh in others:
            send(slot, slot, relay_ss.at[k], grad_rs.at[h, pe], e, wrap(h, dh, halves))
            k += 1
    for dh in [0] + others:
        ph = wrap(h, halves - dh, halves)
        if dh:
            for d in [0] + near:
                pe = flip(e, d)
                arrived(grows.at[ph, pe], grad_rs.at[ph, pe])

        def act_step(cols, size, ph=ph, dh=dh):
            at = pl.ds(pl.multiple_of(ph * width, width), width)
            act = dot_t(grows[ph].reshape(rows, width), wd[cols, at])
            if dh:
                act = act + act_v[:, cols]
            if dh < halves - 1:
                act_v[:, cols] = act
            else:
                gate = gate_v[:, cols]
                sigma = 1.0 / (1.0 + jnp.exp(-gate))
                gg[:, cols] = (
                    act * up_v[:, cols] * sigma * (1.0 + gate * (1.0 - sigma))
                ).astype(jnp.bfloat16)
                gu[:, cols] = (act * gate * sigma).astype(jnp.bfloat16)

        tiles(hidden, act_step)

    for dh in others + [0]:
        ph = wrap(h, dh, halves)

        def back_step(cols, size, ph=ph, dh=dh):
            at = pl.ds(pl.multiple_of(cols.start + ph * width, size), size)
            part = dot_t(gg[...], wg[at, :]) + dot_t(gu[...], wu[at, :])
            part = part.astype(jnp.bfloat16).reshape(chips, 2, tok, size)
            for q in range(2):
                psend[dh, q, :, :, cols] = part[:, q]

        tiles(width, back_step)
        send(psend.at[dh, 1 - parity], prec.at[dh], pair_ss.at[dh], pair_rs.at[dh], sibling, h)
    order = chips_far + [0]
    for dh in others:
        arrived(prec.at[dh], pair_rs.at[dh])
        for j, d in enumerate(order):
            pm = flip(chip, d)
            fsend[dh, pm] = (
                psend[dh, parity, pm].astype(jnp.float32) + prec[dh, pm].astype(jnp.float32)
            ).astype(jnp.bfloat16)
            send(
                fsend.at[dh, pm], frecv.at[halves - dh, pm],
                fpart_ss.at[dh, j], fpart_rs.at[halves - dh, j], e, wrap(h, dh, halves),
            )
    arrived(prec.at[0], pair_rs.at[0])
    for j, d in enumerate(order):
        pm = flip(chip, d)
        total = psend[0, parity, pm].astype(jnp.float32) + prec[0, pm].astype(jnp.float32)
        for dh in others:
            arrived(frecv.at[dh, pm], fpart_rs.at[dh, j])
            total = total + frecv[dh, pm].astype(jnp.float32)
        if d:
            rsend[pm] = total.astype(jnp.bfloat16)
            send(rsend.at[pm], fin.at[chip], fin_ss.at[j], fin_rs.at[chip], 2 * pm + parity, h)
    for d in chips_near:
        pm = flip(chip, d)
        arrived(fin.at[pm], fin_rs.at[pm])
        total = total + fin[pm].astype(jnp.float32)
    gtok_ref[...] = total.astype(jnp.bfloat16)
    for c in sends:
        c.wait_send()


def fused(tokens, upstream, expert_ids, gate_probs, pad_mask, gate_weight, up_weight, down_weight):
    n, halves = lax.axis_size("expert"), lax.axis_size("half")
    tok, width = tokens.shape
    hidden = gate_weight.shape[2]
    rows, full, chips = n * tok, halves * width, n // 2
    top = expert_ids.shape[1]
    low, wide = jnp.bfloat16, jnp.float32
    vmem, dma = pltpu.VMEM, pltpu.SemaphoreType.DMA
    local = pl.BlockSpec(memory_space=pltpu.VMEM)
    remain = pl.BlockSpec(memory_space=pl.ANY)
    result = [jax.ShapeDtypeStruct((tok, width), low)] * 2
    outs = pl.pallas_call(
        functools.partial(fused_kernel, n, halves),
        out_shape=result,
        in_specs=[remain] * 8,
        out_specs=[local] * 2,
        scratch_shapes=[
            vmem((tok, width), low),
            vmem((top, tok), jnp.int32),
            vmem((top, tok), wide),
            vmem((1, tok), jnp.int32),
            vmem((halves, n, tok, width), low),
            vmem((full, hidden), low),
            vmem((full, hidden), low),
            vmem((hidden, full), low),
            vmem((rows, hidden), wide),
            vmem((rows, hidden), wide),
            vmem((rows, hidden), wide),
            vmem((rows, hidden), low),
            vmem((rows, hidden), low),
            vmem((rows, hidden), low),
            vmem((halves, n, tok, width), low),
            vmem((halves, n, tok, width), low),
            vmem((n, tok, width), low),
            vmem((n, tok, width), low),
            vmem((n, tok, width), low),
            vmem((halves, n, rows), wide),
            vmem((n, rows), wide),
            vmem((n, tok, width), low),
            vmem((halves, n, tok, width), low),
            vmem((halves, 2, chips, tok, width), low),
            vmem((halves, chips, tok, width), low),
            vmem((halves, chips, tok, width), low),
            vmem((halves, chips, tok, width), low),
            vmem((chips, tok, width), low),
            vmem((chips, tok, width), low),
            dma((8,)),
            dma((2 * halves * n,)),
            dma((halves, n)),
            dma((halves, n)),
            dma((halves, n)),
            dma((n,)),
            dma((n,)),
            dma((halves,)),
            dma((halves,)),
            dma((n,)),
            dma((halves, n)),
            dma((halves * n,)),
            dma((halves,)),
            dma((halves,)),
            dma((halves, chips)),
            dma((halves, chips)),
            dma((chips,)),
            dma((chips,)),
        ],
        compiler_params=pltpu.CompilerParams(
            collective_id=0, has_side_effects=True, vmem_limit_bytes=56 * 1024 * 1024
        ),
        name="experts",
    )(
        tokens, upstream, expert_ids.T, gate_probs.T, pad_mask.reshape(1, tok),
        gate_weight, up_weight, down_weight,
    )
    return pl.pallas_call(
        copy_kernel, out_shape=result, in_specs=[local] * 2, out_specs=[local] * 2, name="results"
    )(*outs)


def shards(tokens, upstream, expert_ids, gate_probs, pad_mask, gate_weight, up_weight, down_weight):
    tok_count, top_count = expert_ids.shape
    experts = lax.axis_size("expert")
    capacity = min(tok_count, 2 * tok_count * top_count // experts)
    if capacity == tok_count and experts > 1 and experts & (experts - 1) == 0:
        return fused(
            tokens, upstream, expert_ids, gate_probs, pad_mask, gate_weight, up_weight, down_weight
        )
    slots_total = experts * capacity
    full_width = tokens.shape[1] * lax.axis_size("half")
    slot_dest = assign_slots(expert_ids, experts, capacity)
    place_items = placement_matrix(slot_dest, slots_total)
    place_tokens = jnp.sum(place_items.reshape(slots_total, tok_count, top_count), axis=2)
    weight_gate = gate_weight[0]
    weight_up = up_weight[0]
    weight_down = down_weight[0]
    rows_in = to_experts(place_tokens, tokens)
    gate_val = jnp.dot(rows_in, weight_gate, preferred_element_type=jnp.float32)
    up_val = jnp.dot(rows_in, weight_up, preferred_element_type=jnp.float32)
    hidden_act = (jax.nn.silu(gate_val) * up_val).astype(jnp.bfloat16)
    partial_value = jnp.dot(hidden_act, weight_down, preferred_element_type=jnp.float32)
    out_home = to_homes(partial_value)
    outputs = jnp.take(out_home, slot_dest, axis=0).reshape(tok_count, top_count, -1)
    out_float = outputs.astype(jnp.float32)
    shares = gate_probs / jnp.sum(gate_probs, axis=1, keepdims=True)
    layer_out = jnp.sum(shares[:, :, None] * out_float, axis=1).astype(jnp.bfloat16)
    gram_part = jnp.einsum("tjd,tkd->tjk", out_float, out_float) / math.sqrt(full_width)
    gram = lax.psum(gram_part, "half")
    off_diag = 1.0 - jnp.eye(top_count, dtype=jnp.float32)
    coeffs = orth_weight * gram * off_diag
    grad_out = pad_mask.astype(jnp.float32)[:, None, None] * (
        shares[:, :, None] * upstream.astype(jnp.float32)[:, None, :]
        + jnp.einsum("tjk,tkd->tjd", coeffs, out_float)
    )
    grad_items = grad_out.astype(jnp.bfloat16).reshape(tok_count * top_count, -1)
    grad_rows = to_experts(place_items, grad_items)
    grad_act = jnp.einsum("rd,hd->rh", grad_rows, weight_down, preferred_element_type=jnp.float32)
    sigma = jax.nn.sigmoid(gate_val)
    grad_gate = (grad_act * up_val * sigma * (1.0 + gate_val * (1.0 - sigma))).astype(jnp.bfloat16)
    grad_up = (grad_act * gate_val * sigma).astype(jnp.bfloat16)
    grad_partial = jnp.einsum(
        "rh,dh->rd", grad_gate, weight_gate, preferred_element_type=jnp.float32
    )
    grad_partial = grad_partial + jnp.einsum(
        "rh,dh->rd", grad_up, weight_up, preferred_element_type=jnp.float32
    )
    grad_home = to_homes(grad_partial)
    grad_pairs = jnp.take(grad_home, slot_dest, axis=0).reshape(tok_count, top_count, -1)
    grad_tokens = jnp.sum(grad_pairs.astype(jnp.float32), axis=1).astype(jnp.bfloat16)
    return (layer_out, grad_tokens)


def solution(mesh):
    in_specs = (
        P("expert", "half"),
        P("expert", "half"),
        P("expert", None),
        P("expert", None),
        P("expert"),
        P("expert", None, "half"),
        P("expert", None, "half"),
        P("expert", "half", None),
    )
    out_specs = (P("expert", "half"), P("expert", "half"))
    return jax.shard_map(shards, mesh=mesh, in_specs=in_specs, out_specs=out_specs, check_vma=False)
```

profile of v0, /device:TPU:0, one launch (start us, length us, event | category | flops | bytes accessed | tf_op | source)
XLA Modules:
  0.0 78.3 jit_solution(13308271119655710484)
XLA Ops:
  0.6 76.2 %experts.1 = (bf16[16,1024]{1,0:T(8,128)(2,1)}, bf16[16,1024]{1,0:T(8,128)(2,1)}) custom-call(bf16[16,1024]{1,0:T(8,128)(2,1)} %tok_hbm.1, bf16[16,1024]{1,0:T(8,128)(2,1)} %up_hbm.1, s32[8,16]{1,0:T(8,128)} %bitcast.3, f32[8,16]{1,0:T(8,128)} %bitcast.4, s32[1,16]{1,0:T(1,128)} %bitcast.5, bf16[1,2048,768]{2,1,0:T(8,128)(2,1)} %wg_hbm.1, ...), custom_call_target="tpu_custom_call" | custom-call | tf_op jit(solution)/shard_map/experts/pallas_call | solution.py:385
  76.9 1.4 %results.1 = (bf16[16,1024]{1,0:T(8,128)(2,1)}, bf16[16,1024]{1,0:T(8,128)(2,1)}) custom-call(bf16[16,1024]{1,0:T(8,128)(2,1)} %get-tuple-element.4.a_ref, bf16[16,1024]{1,0:T(8,128)(2,1)} %get-tuple-element.5.b_ref), custom_call_target="tpu_custom_call" | custom-call | tf_op jit(solution)/shard_map/results/pallas_call | solution.py:447
where the time goes:
time: 78.5 us; the launch traced here: 78.3 us
  Pallas kernels  77.6 us (99%)
    pallas_call x1, Pallas kernels, fused(): pl.pallas_call(functools.partial(fused_kernel, n, halves), out_shape=resu...  76.2 us

commit v1 on v0

--- a/solution.py
+++ b/solution.py
@@ -38,12 +38,12 @@
     return lax.all_to_all(summed, "expert", split_axis=0, concat_axis=0, tiled=True)
 
 
-def block_of(width):
-    return next((b for b in (256, 128) if width % b == 0), width)
-
-
-def tiles(width, body):
-    size = block_of(width)
+def block_of(width, most):
+    return next((b for b in (1024, 512, 256, 128) if b <= most and width % b == 0), width)
+
+
+def tiles(width, body, most=256):
+    size = block_of(width, most)
 
     def step(j, carry):
         body(pl.ds(pl.multiple_of(j * size, size), size), size)
@@ -201,7 +201,7 @@
             part = dot(hid[...], wd[:, at])
             osend[dh, :, :, cols] = part.reshape(n, tok, size).astype(jnp.bfloat16)
 
-        tiles(width, down_step)
+        tiles(width, down_step, 1024)
         if dh:
             for j, d in enumerate(outer + [0]):
                 pe = flip(e, d)
@@ -338,7 +338,7 @@
             for q in range(2):
                 psend[dh, q, :, :, cols] = part[:, q]
 
-        tiles(width, back_step)
+        tiles(width, back_step, 1024)
         send(psend.at[dh, 1 - parity], prec.at[dh], pair_ss.at[dh], pair_rs.at[dh], sibling, h)
     order = chips_far + [0]
     for dh in others:

time: 78.5 us -> 77.7 us (0.990)
  Pallas kernels: 77.6 us -> 76.8 us
    pallas_call x1, Pallas kernels: 76.2 us -> 75.4 us  [fused(): pl.pallas_call(functools.partial(fused_kernel, n, halves), out_shape=resu...]
where the time goes in v1:
time: 77.7 us; the launch traced here: 77.5 us
  Pallas kernels  76.8 us (99%)
    pallas_call x1, Pallas kernels, fused(): pl.pallas_call(functools.partial(fused_kernel, n, halves), out_shape=resu...  75.4 us

profile of v1, /device:TPU:0, one launch (start us, length us, event | category | flops | bytes accessed | tf_op | source)
XLA Modules:
  0.0 77.5 jit_solution(13987203245240734043)
XLA Ops:
  0.6 75.4 %experts.1 = (bf16[16,1024]{1,0:T(8,128)(2,1)}, bf16[16,1024]{1,0:T(8,128)(2,1)}) custom-call(bf16[16,1024]{1,0:T(8,128)(2,1)} %tok_hbm.1, bf16[16,1024]{1,0:T(8,128)(2,1)} %up_hbm.1, s32[8,16]{1,0:T(8,128)} %bitcast.3, f32[8,16]{1,0:T(8,128)} %bitcast.4, s32[1,16]{1,0:T(1,128)} %bitcast.5, bf16[1,2048,768]{2,1,0:T(8,128)(2,1)} %wg_hbm.1, ...), custom_call_target="tpu_custom_call" | custom-call | tf_op jit(solution)/shard_map/experts/pallas_call | solution.py:385
  76.1 1.4 %results.1 = (bf16[16,1024]{1,0:T(8,128)(2,1)}, bf16[16,1024]{1,0:T(8,128)(2,1)}) custom-call(bf16[16,1024]{1,0:T(8,128)(2,1)} %get-tuple-element.4.a_ref, bf16[16,1024]{1,0:T(8,128)(2,1)} %get-tuple-element.5.b_ref), custom_call_target="tpu_custom_call" | custom-call | tf_op jit(solution)/shard_map/results/pallas_call | solution.py:447

commit v2 on v1

v2 whole, which is shorter than its diff:
```python
import functools
import math

import jax
import jax.numpy as jnp
from jax import lax
from jax.experimental import pallas as pl
from jax.experimental.pallas import tpu as pltpu
from jax.sharding import PartitionSpec as P

orth_weight = 0.25


def assign_slots(expert_ids, experts, capacity):
    tok_count, top_count = expert_ids.shape
    flat_ids = expert_ids.reshape(tok_count * top_count)
    onehot = (flat_ids[:, None] == jnp.arange(experts, dtype=jnp.int32)[None, :]).astype(jnp.int32)
    before = jnp.cumsum(onehot, axis=0) - onehot
    slot_index = jnp.sum(before * onehot, axis=1)
    return flat_ids * capacity + slot_index


def placement_matrix(slot_dest, slots_total):
    row_index = jnp.arange(slots_total, dtype=jnp.int32)
    return (row_index[:, None] == slot_dest[None, :]).astype(jnp.bfloat16)


def to_experts(place, items):
    whole = lax.all_gather(items, "half", axis=1, tiled=True)
    buckets = jnp.dot(place, whole, preferred_element_type=jnp.float32).astype(jnp.bfloat16)
    return lax.all_to_all(buckets, "expert", split_axis=0, concat_axis=0, tiled=True)


def to_homes(partial_value):
    summed = lax.psum_scatter(
        partial_value.astype(jnp.bfloat16), "half", scatter_dimension=1, tiled=True
    )
    return lax.all_to_all(summed, "expert", split_axis=0, concat_axis=0, tiled=True)


def block_of(width, most):
    return next((b for b in (1024, 512, 256, 128) if b <= most and width % b == 0), width)


def tiles(width, body, most=256):
    size = block_of(width, most)

    def step(j, carry):
        body(pl.ds(pl.multiple_of(j * size, size), size), size)
        return carry

    lax.fori_loop(0, width // size, step, 0)


def dot(a, b):
    return jnp.dot(a, b, preferred_element_type=jnp.float32)


def dot_t(a, b):
    return lax.dot_general(a, b, (((1,), (1,)), ((), ())), preferred_element_type=jnp.float32)


def copy_kernel(a_ref, b_ref, a_out, b_out):
    a_out[...] = a_ref[...]
    b_out[...] = b_ref[...]


def fused_kernel(
    n, groups,
    tok_hbm, up_hbm, ids_hbm, probs_hbm, pad_hbm, wg_hbm, wu_hbm, wd_hbm,
    layer_ref, gtok_ref,
    up_ref, ids_ref, probs_ref, pad_ref,
    tok_buf, wg, wu, wd, gate_v, up_v, act_v, hid, gg, gu,
    osend, orecv, ored, xrecv, xs, gram_s, share_s, gsend, grows, psend, prec, fsend, frecv, rsend, fin,
    w_sem, plane_ss, cross_ss, twin_ss, tok_rs, twin_rs, part_ss, part_rs, out_ss, out_rs, gram_ss, gram_rs,
    grad_ss, grad_rs, relay_ss, relay_rs, pair_ss, pair_rs, fpart_ss, fpart_rs, fin_ss, fin_rs,
):
    e = lax.axis_index("expert")
    h = lax.axis_index("half")
    sub, width = tok_buf.shape[3:]
    hidden = wg.shape[1]
    tok = groups * sub
    rows = n * sub
    chips = n // 2
    parity = lax.rem(e, 2)
    chip = lax.div(e, 2)
    sibling = e + 1 - 2 * parity
    other = 1 - h
    full = 2 * width

    def remote(src, dst, ssem, rsem, pe, ph):
        return pltpu.make_async_remote_copy(
            src_ref=src, dst_ref=dst, send_sem=ssem, recv_sem=rsem,
            device_id=(pe, ph), device_id_type=pl.DeviceIdType.MESH,
        )

    def send(*args):
        remote(*args).start()

    def flip(a, d):
        bit = 1
        out = a
        while bit <= d:
            if d & bit:
                out = out + bit * (1 - 2 * lax.rem(lax.div(a, bit), 2))
            bit *= 2
        return out

    def arrived(slot, rsem):
        remote(slot, slot, pair_ss.at[0], rsem, sibling, h).wait_recv()

    def drained(sent, ssem):
        remote(sent, sent, ssem, pair_rs.at[0], sibling, h).wait_send()

    moves = [(tok_hbm.at[pl.ds(g * sub, sub)], tok_buf.at[g, h, e]) for g in range(groups)]
    moves += [(ids_hbm, ids_ref), (probs_hbm, probs_ref), (pad_hbm, pad_ref)]
    moves += [(up_hbm.at[pl.ds(g * sub, sub)], up_ref.at[g]) for g in range(groups)]
    moves += [(wg_hbm.at[0], wg), (wu_hbm.at[0], wu), (wd_hbm.at[0], wd)]
    loads = [pltpu.make_async_copy(src, dst, w_sem.at[i]) for i, (src, dst) in enumerate(moves)]
    for c in loads:
        c.start()

    near = list(range(1, n))
    outer = near[::-1]
    chips_near = list(range(1, chips))
    chips_far = chips_near[::-1]

    barrier = pltpu.get_barrier_semaphore()
    for d in outer:
        pl.semaphore_signal(
            barrier, inc=1, device_id=(flip(e, d), h), device_id_type=pl.DeviceIdType.MESH
        )
    pl.semaphore_signal(barrier, inc=1, device_id=(e, other), device_id_type=pl.DeviceIdType.MESH)
    pl.semaphore_wait(barrier, n)

    def peer(d):
        return 2 * flip(chip, d) + parity

    for g in range(groups):
        loads[g].wait()
        mine = tok_buf.at[g, h, e]
        for d in chips_far:
            send(mine, mine, plane_ss.at[g], tok_rs.at[g, h, e], peer(d), h)
        send(mine, mine, cross_ss.at[g], tok_rs.at[g, h, e], e, other)
        send(mine, mine, twin_ss.at[g], twin_rs.at[g, h], sibling, h)

    for c in loads[groups:-3]:
        c.wait()
    eye = (
        lax.broadcasted_iota(jnp.int32, (tok, tok), 0)
        == lax.broadcasted_iota(jnp.int32, (tok, tok), 1)
    )
    top = ids_ref.shape[0]
    lane = lax.broadcasted_iota(jnp.int32, (tok, top), 1)

    def column(row):
        return jnp.sum(jnp.where(eye, jnp.broadcast_to(row, (tok, tok)), 0.0), axis=1, keepdims=True)

    ids = jnp.zeros((tok, top), jnp.float32)
    probs = jnp.zeros((tok, top), jnp.float32)
    for j in range(top):
        ids = jnp.where(lane == j, column(ids_ref[j:j + 1, :].astype(jnp.float32)), ids)
        probs = jnp.where(lane == j, column(probs_ref[j:j + 1, :]), probs)
    pad = column(pad_ref[...].astype(jnp.float32))
    shares = probs / jnp.sum(probs, axis=1, keepdims=True)
    for i in range(n):
        share = jnp.sum(jnp.where(ids == float(i), shares, 0.0), axis=1, keepdims=True)
        share_s[i] = jnp.broadcast_to(share, (tok, share_s.shape[2]))

    for g in range(groups):
        for d in chips_near:
            slot = tok_buf.at[g, h, peer(d)]
            arrived(slot, tok_rs.at[g, h, peer(d)])
            send(slot, slot, cross_ss.at[g], tok_rs.at[g, h, peer(d)], e, other)
            send(slot, slot, twin_ss.at[g], twin_rs.at[g, h], sibling, h)

    def gathered(g):
        for d in [0] + chips_near:
            slot = tok_buf.at[g, other, peer(d)]
            arrived(slot, tok_rs.at[g, other, peer(d)])
            send(slot, slot, twin_ss.at[g], twin_rs.at[g, other], sibling, h)
        for ph in range(2):
            arrived(tok_buf.at[g, ph, pl.ds(0, chips)], twin_rs.at[g, ph])

    def hidden_rows(g):
        at = pl.ds(g * rows, rows)

        def hidden_step(cols, size):
            gate = up = None
            for ph in range(2):
                depth = pl.ds(ph * width, width)
                x = tok_buf[g, ph].reshape(rows, width)
                gate_part = dot(x, wg[depth, cols])
                up_part = dot(x, wu[depth, cols])
                gate = gate_part if gate is None else gate + gate_part
                up = up_part if up is None else up + up_part
            gate_v[at, cols] = gate
            up_v[at, cols] = up
            hid[at, cols] = (gate / (1.0 + jnp.exp(-gate)) * up).astype(jnp.bfloat16)

        tiles(hidden, hidden_step)

    def down(g, far):
        start = (other if far else h) * width

        def down_step(cols, size):
            at = pl.ds(pl.multiple_of(cols.start + start, size), size)
            part = dot(hid[pl.ds(g * rows, rows), :], wd[:, at])
            osend[g, far, :, :, cols] = part.reshape(n, sub, size).astype(jnp.bfloat16)

        tiles(width, down_step, 1024)

    def cross_parts(g):
        for d in outer + [0]:
            pe = flip(e, d)
            send(osend.at[g, 1, pe], orecv.at[g, pe], part_ss.at[g], part_rs.at[g, pe], e, other)

    def forward(g, first, last):
        for d in (outer + [0])[first:last]:
            pe = flip(e, d)
            arrived(orecv.at[g, pe], part_rs.at[g, pe])
            total = osend[g, 0, pe].astype(jnp.float32) + orecv[g, pe].astype(jnp.float32)
            total = total.astype(jnp.bfloat16)
            if d:
                ored[g, pe] = total
                send(ored.at[g, pe], xrecv.at[g, e], out_ss.at[g], out_rs.at[g, e], pe, h)
            else:
                xrecv[g, e] = total

    same = (
        lax.rem(lax.broadcasted_iota(jnp.int32, (sub, rows), 1), sub)
        == lax.broadcasted_iota(jnp.int32, (sub, rows), 0)
    ).astype(jnp.float32)
    apart = (
        lax.div(lax.broadcasted_iota(jnp.int32, (n, rows), 1), sub)
        != lax.broadcasted_iota(jnp.int32, (n, rows), 0)
    ).astype(jnp.float32)

    def share_of(g, i):
        return share_s[i, pl.ds(g * sub, sub), :][:, :1]

    def products(g):
        layer = jnp.zeros((sub, width), jnp.float32)
        for d in [0] + near:
            pe = flip(e, d)
            share = share_of(g, pe)
            if d:
                arrived(xrecv.at[g, pe], out_rs.at[g, pe])
            value = jnp.where(share > 0.0, xrecv[g, pe].astype(jnp.float32), 0.0)
            xs[g, pe] = value.astype(jnp.bfloat16)
            layer = layer + share * value
        x_all = xs[g].reshape(rows, width)
        gram = dot_t(x_all, x_all).reshape(n, sub, rows) * same[None]
        gram_s[g, h] = jnp.sum(gram, axis=1)
        send(gram_s.at[g, h], gram_s.at[g, h], gram_ss.at[g], gram_rs.at[g], e, other)
        return layer

    def mix(g):
        arrived(gram_s.at[g, other], gram_rs.at[g])
        whole = (gram_s[g, 0] + gram_s[g, 1]) * (apart * (orth_weight / math.sqrt(full)))
        x_all = xs[g].reshape(rows, width)
        coeffs = (whole[:, None, :] * same[None]).reshape(rows, rows)
        high = coeffs.astype(jnp.bfloat16)
        low = (coeffs - high.astype(jnp.float32)).astype(jnp.bfloat16)
        mixed = (dot(high, x_all) + dot(low, x_all)).reshape(n, sub, width)
        upstream = up_ref[g].astype(jnp.float32)
        real = pad[g * sub:(g + 1) * sub]
        for i in range(n):
            gsend[g, i] = (real * (share_of(g, i) * upstream + mixed[i])).astype(jnp.bfloat16)
        for d in near:
            pe = flip(e, d)
            send(gsend.at[g, pe], grows.at[h, g, e], grad_ss.at[g], grad_rs.at[g, e], pe, h)
        send(gsend.at[g, e], grows.at[h, g, e], relay_ss.at[g], relay_rs.at[g], e, other)
        grows[h, g, e] = gsend[g, e]

    def relay(g, first, last):
        for d in near[first:last]:
            pe = flip(e, d)
            slot = grows.at[h, g, pe]
            arrived(slot, grad_rs.at[g, pe])
            send(slot, slot, relay_ss.at[g], relay_rs.at[g], e, other)

    gathered(0)
    for c in loads[-3:-1]:
        c.wait()
    hidden_rows(0)
    loads[-1].wait()
    down(0, 1)
    cross_parts(0)
    gathered(1)
    hidden_rows(1)
    down(1, 1)
    cross_parts(1)
    down(0, 0)
    down(1, 0)
    forward(0, 0, n)
    forward(1, 0, n // 4)
    layer_a = products(0)
    forward(1, n // 4, 9 * n // 16)
    mix(0)
    forward(1, 9 * n // 16, n)
    layer_b = products(1)
    relay(0, 0, n // 4)
    mix(1)
    layer_ref[...] = jnp.concatenate([layer_a, layer_b], axis=0).astype(jnp.bfloat16)
    relay(0, n // 4, n - 1)
    relay(1, 0, n - 1)

    for dh in range(2):
        ph = lax.rem(h + dh, 2)
        if dh:
            for g in range(groups):
                arrived(grows.at[other, g], relay_rs.at[g])

        def act_step(cols, size, ph=ph, dh=dh):
            at = pl.ds(pl.multiple_of(ph * width, width), width)
            act = dot_t(grows[ph].reshape(groups * rows, width), wd[cols, at])
            if dh:
                act = act + act_v[:, cols]
                gate = gate_v[:, cols]
                sigma = 1.0 / (1.0 + jnp.exp(-gate))
                gg[:, cols] = (
                    act * up_v[:, cols] * sigma * (1.0 + gate * (1.0 - sigma))
                ).astype(jnp.bfloat16)
                gu[:, cols] = (act * gate * sigma).astype(jnp.bfloat16)
            else:
                act_v[:, cols] = act

        tiles(hidden, act_step)

    for far in (1, 0):
        start = (other if far else h) * width

        def back_step(cols, size, start=start, far=far):
            at = pl.ds(pl.multiple_of(cols.start + start, size), size)
            part = dot_t(gg[...], wg[at, :]) + dot_t(gu[...], wu[at, :])
            part = part.astype(jnp.bfloat16).reshape(groups, chips, 2, sub, size)
            for g in range(groups):
                for q in range(2):
                    psend[far, q, :, g, :, cols] = part[g, :, q]

        tiles(width, back_step, 1024)
        send(psend.at[far, 1 - parity], prec.at[far], pair_ss.at[far], pair_rs.at[far], sibling, h)
    order = chips_far + [0]
    arrived(prec.at[1], pair_rs.at[1])
    for d in order:
        pm = flip(chip, d)
        fsend[pm] = (
            psend[1, parity, pm].astype(jnp.float32) + prec[1, pm].astype(jnp.float32)
        ).astype(jnp.bfloat16)
        send(fsend.at[pm], frecv.at[pm], fpart_ss, fpart_rs.at[pm], e, other)
    arrived(prec.at[0], pair_rs.at[0])
    for d in order:
        pm = flip(chip, d)
        total = psend[0, parity, pm].astype(jnp.float32) + prec[0, pm].astype(jnp.float32)
        arrived(frecv.at[pm], fpart_rs.at[pm])
        total = total + frecv[pm].astype(jnp.float32)
        if d:
            rsend[pm] = total.astype(jnp.bfloat16)
            send(rsend.at[pm], fin.at[chip], fin_ss, fin_rs.at[chip], peer(d), h)
    for d in chips_near:
        pm = flip(chip, d)
        arrived(fin.at[pm], fin_rs.at[pm])
        total = total + fin[pm].astype(jnp.float32)
    gtok_ref[...] = total.reshape(tok, width).astype(jnp.bfloat16)
    for g in range(groups):
        drained(tok_buf.at[g, 0, pl.ds(0, chips - 1)], plane_ss.at[g])
        drained(tok_buf.at[g, 0, pl.ds(0, chips)], cross_ss.at[g])
        drained(tok_buf.at[g, 0], twin_ss.at[g])
        drained(osend.at[g, 1], part_ss.at[g])
        drained(ored.at[g, pl.ds(0, n - 1)], out_ss.at[g])
        drained(gram_s.at[g, 0], gram_ss.at[g])
        drained(gsend.at[g, pl.ds(0, n - 1)], grad_ss.at[g])
        drained(grows.at[0, g], relay_ss.at[g])
    for far in range(2):
        drained(psend.at[far, 0], pair_ss.at[far])
    drained(fsend, fpart_ss)
    drained(rsend.at[pl.ds(0, chips - 1)], fin_ss)


def fused(tokens, upstream, expert_ids, gate_probs, pad_mask, gate_weight, up_weight, down_weight):
    n, groups = lax.axis_size("expert"), 2
    tok, width = tokens.shape
    hidden = gate_weight.shape[2]
    sub, full, chips = tok // groups, 2 * width, n // 2
    every = n * tok
    top = expert_ids.shape[1]
    low, wide = jnp.bfloat16, jnp.float32
    vmem, dma = pltpu.VMEM, pltpu.SemaphoreType.DMA
    local = pl.BlockSpec(memory_space=pltpu.VMEM)
    remain = pl.BlockSpec(memory_space=pl.ANY)
    result = [jax.ShapeDtypeStruct((tok, width), low)] * 2
    outs = pl.pallas_call(
        functools.partial(fused_kernel, n, groups),
        out_shape=result,
        in_specs=[remain] * 8,
        out_specs=[local] * 2,
        scratch_shapes=[
            vmem((groups, sub, width), low),
            vmem((top, tok), jnp.int32),
            vmem((top, tok), wide),
            vmem((1, tok), jnp.int32),
            vmem((groups, 2, n, sub, width), low),
            vmem((full, hidden), low),
            vmem((full, hidden), low),
            vmem((hidden, full), low),
            vmem((every, hidden), wide),
            vmem((every, hidden), wide),
            vmem((every, hidden), wide),
            vmem((every, hidden), low),
            vmem((every, hidden), low),
            vmem((every, hidden), low),
            vmem((groups, 2, n, sub, width), low),
            vmem((groups, n, sub, width), low),
            vmem((groups, n, sub, width), low),
            vmem((groups, n, sub, width), low),
            vmem((groups, n, sub, width), low),
            vmem((groups, 2, n, n * sub), wide),
            vmem((n, tok, 128), wide),
            vmem((groups, n, sub, width), low),
            vmem((2, groups, n, sub, width), low),
            vmem((2, 2, chips, groups, sub, width), low),
            vmem((2, chips, groups, sub, width), low),
            vmem((chips, groups, sub, width), low),
            vmem((chips, groups, sub, width), low),
            vmem((chips, groups, sub, width), low),
            vmem((chips, groups, sub, width), low),
            dma((2 * groups + 6,)),
            dma((groups,)),
            dma((groups,)),
            dma((groups,)),
            dma((groups, 2, n)),
            dma((groups, 2)),
            dma((groups,)),
            dma((groups, n)),
            dma((groups,)),
            dma((groups, n)),
            dma((groups,)),
            dma((groups,)),
            dma((groups,)),
            dma((groups, n)),
            dma((groups,)),
            dma((groups,)),
            dma((2,)),
            dma((2,)),
            dma(()),
            dma((chips,)),
            dma(()),
            dma((chips,)),
        ],
        compiler_params=pltpu.CompilerParams(
            collective_id=0, has_side_effects=True, vmem_limit_bytes=56 * 1024 * 1024
        ),
        name="experts",
    )(
        tokens, upstream, expert_ids.T, gate_probs.T, pad_mask.reshape(1, tok),
        gate_weight, up_weight, down_weight,
    )
    return pl.pallas_call(
        copy_kernel, out_shape=result, in_specs=[local] * 2, out_specs=[local] * 2, name="results"
    )(*outs)


def shards(tokens, upstream, expert_ids, gate_probs, pad_mask, gate_weight, up_weight, down_weight):
    tok_count, top_count = expert_ids.shape
    experts = lax.axis_size("expert")
    capacity = min(tok_count, 2 * tok_count * top_count // experts)
    paired = experts > 3 and experts & (experts - 1) == 0 and lax.axis_size("half") == 2
    if capacity == tok_count and tok_count % 16 == 0 and paired:
        return fused(
            tokens, upstream, expert_ids, gate_probs, pad_mask, gate_weight, up_weight, down_weight
        )
    slots_total = experts * capacity
    full_width = tokens.shape[1] * lax.axis_size("half")
    slot_dest = assign_slots(expert_ids, experts, capacity)
    place_items = placement_matrix(slot_dest, slots_total)
    place_tokens = jnp.sum(place_items.reshape(slots_total, tok_count, top_count), axis=2)
    weight_gate = gate_weight[0]
    weight_up = up_weight[0]
    weight_down = down_weight[0]
    rows_in = to_experts(place_tokens, tokens)
    gate_val = jnp.dot(rows_in, weight_gate, preferred_element_type=jnp.float32)
    up_val = jnp.dot(rows_in, weight_up, preferred_element_type=jnp.float32)
    hidden_act = (jax.nn.silu(gate_val) * up_val).astype(jnp.bfloat16)
    partial_value = jnp.dot(hidden_act, weight_down, preferred_element_type=jnp.float32)
    out_home = to_homes(partial_value)
    outputs = jnp.take(out_home, slot_dest, axis=0).reshape(tok_count, top_count, -1)
    out_float = outputs.astype(jnp.float32)
    shares = gate_probs / jnp.sum(gate_probs, axis=1, keepdims=True)
    layer_out = jnp.sum(shares[:, :, None] * out_float, axis=1).astype(jnp.bfloat16)
    gram_part = jnp.einsum("tjd,tkd->tjk", out_float, out_float) / math.sqrt(full_width)
    gram = lax.psum(gram_part, "half")
    off_diag = 1.0 - jnp.eye(top_count, dtype=jnp.float32)
    coeffs = orth_weight * gram * off_diag
    grad_out = pad_mask.astype(jnp.float32)[:, None, None] * (
        shares[:, :, None] * upstream.astype(jnp.float32)[:, None, :]
        + jnp.einsum("tjk,tkd->tjd", coeffs, out_float)
    )
    grad_items = grad_out.astype(jnp.bfloat16).reshape(tok_count * top_count, -1)
    grad_rows = to_experts(place_items, grad_items)
    grad_act = jnp.einsum("rd,hd->rh", grad_rows, weight_down, preferred_element_type=jnp.float32)
    sigma = jax.nn.sigmoid(gate_val)
    grad_gate = (grad_act * up_val * sigma * (1.0 + gate_val * (1.0 - sigma))).astype(jnp.bfloat16)
    grad_up = (grad_act * gate_val * sigma).astype(jnp.bfloat16)
    grad_partial = jnp.einsum(
        "rh,dh->rd", grad_gate, weight_gate, preferred_element_type=jnp.float32
    )
    grad_partial = grad_partial + jnp.einsum(
        "rh,dh->rd", grad_up, weight_up, preferred_element_type=jnp.float32
    )
    grad_home = to_homes(grad_partial)
    grad_pairs = jnp.take(grad_home, slot_dest, axis=0).reshape(tok_count, top_count, -1)
    grad_tokens = jnp.sum(grad_pairs.astype(jnp.float32), axis=1).astype(jnp.bfloat16)
    return (layer_out, grad_tokens)


def solution(mesh):
    in_specs = (
        P("expert", "half"),
        P("expert", "half"),
        P("expert", None),
        P("expert", None),
        P("expert"),
        P("expert", None, "half"),
        P("expert", None, "half"),
        P("expert", "half", None),
    )
    out_specs = (P("expert", "half"), P("expert", "half"))
    return jax.shard_map(shards, mesh=mesh, in_specs=in_specs, out_specs=out_specs, check_vma=False)
```

time: 77.7 us -> 75 us (0.965)
  Pallas kernels: 76.8 us -> 74.2 us
    pallas_call x1, Pallas kernels: 75.4 us -> 72.8 us  [fused(): pl.pallas_call(functools.partial(fused_kernel, n, groups), out_shape=resu...]
where the time goes in v2:
time: 75 us; the launch traced here: 74.8 us
  Pallas kernels  74.2 us (99%)
    pallas_call x1, Pallas kernels, fused(): pl.pallas_call(functools.partial(fused_kernel, n, groups), out_shape=resu...  72.8 us

profile of v2, /device:TPU:0, one launch (start us, length us, event | category | flops | bytes accessed | tf_op | source)
XLA Modules:
  0.0 74.8 jit_solution(8050330077370577998)
XLA Ops:
  0.6 72.8 %experts.1 = (bf16[16,1024]{1,0:T(8,128)(2,1)}, bf16[16,1024]{1,0:T(8,128)(2,1)}) custom-call(bf16[16,1024]{1,0:T(8,128)(2,1)} %tok_hbm.1, bf16[16,1024]{1,0:T(8,128)(2,1)} %up_hbm.1, s32[8,16]{1,0:T(8,128)} %bitcast.3, f32[8,16]{1,0:T(8,128)} %bitcast.4, s32[1,16]{1,0:T(1,128)} %bitcast.5, bf16[1,2048,768]{2,1,0:T(8,128)(2,1)} %wg_hbm.1, ...), custom_call_target="tpu_custom_call" | custom-call | tf_op jit(solution)/shard_map/experts/pallas_call | solution.py:393
  73.4 1.4 %results.1 = (bf16[16,1024]{1,0:T(8,128)(2,1)}, bf16[16,1024]{1,0:T(8,128)(2,1)}) custom-call(bf16[16,1024]{1,0:T(8,128)(2,1)} %get-tuple-element.4.a_ref, bf16[16,1024]{1,0:T(8,128)(2,1)} %get-tuple-element.5.b_ref), custom_call_target="tpu_custom_call" | custom-call | tf_op jit(solution)/shard_map/results/pallas_call | solution.py:459

commit v3 on v2

v3 whole, which is shorter than its diff:
```python
import functools
import math

import jax
import jax.numpy as jnp
from jax import lax
from jax.experimental import pallas as pl
from jax.experimental.pallas import tpu as pltpu
from jax.sharding import PartitionSpec as P

orth_weight = 0.25


def assign_slots(expert_ids, experts, capacity):
    tok_count, top_count = expert_ids.shape
    flat_ids = expert_ids.reshape(tok_count * top_count)
    onehot = (flat_ids[:, None] == jnp.arange(experts, dtype=jnp.int32)[None, :]).astype(jnp.int32)
    before = jnp.cumsum(onehot, axis=0) - onehot
    slot_index = jnp.sum(before * onehot, axis=1)
    return flat_ids * capacity + slot_index


def placement_matrix(slot_dest, slots_total):
    row_index = jnp.arange(slots_total, dtype=jnp.int32)
    return (row_index[:, None] == slot_dest[None, :]).astype(jnp.bfloat16)


def to_experts(place, items):
    whole = lax.all_gather(items, "half", axis=1, tiled=True)
    buckets = jnp.dot(place, whole, preferred_element_type=jnp.float32).astype(jnp.bfloat16)
    return lax.all_to_all(buckets, "expert", split_axis=0, concat_axis=0, tiled=True)


def to_homes(partial_value):
    summed = lax.psum_scatter(
        partial_value.astype(jnp.bfloat16), "half", scatter_dimension=1, tiled=True
    )
    return lax.all_to_all(summed, "expert", split_axis=0, concat_axis=0, tiled=True)


def block_of(width, most):
    return next((b for b in (1024, 512, 256, 128) if b <= most and width % b == 0), width)


def tiles(width, body, most=256):
    size = block_of(width, most)

    def step(j, carry):
        body(pl.ds(pl.multiple_of(j * size, size), size), size)
        return carry

    lax.fori_loop(0, width // size, step, 0)


def dot(a, b):
    return jnp.dot(a, b, preferred_element_type=jnp.float32)


def dot_t(a, b):
    return lax.dot_general(a, b, (((1,), (1,)), ((), ())), preferred_element_type=jnp.float32)


def copy_kernel(a_ref, b_ref, a_out, b_out):
    a_out[...] = a_ref[...]
    b_out[...] = b_ref[...]


def fused_kernel(
    n, groups,
    tok_hbm, up_hbm, ids_hbm, probs_hbm, pad_hbm, wg_hbm, wu_hbm, wd_hbm,
    layer_ref, gtok_ref,
    up_ref, ids_ref, probs_ref, pad_ref,
    tok_buf, wg, wu, wd, gate_v, up_v, act_v, hid, gg, gu,
    osend, orecv, ored, xrecv, xs, gram_s, share_s, gsend, grows, psend, prec, fsend, frecv, rsend, fin,
    w_sem, line_ss, quad_ss, twin_ss, line_rs, quad_rs, twin_rs, part_ss, part_rs, out_ss, out_rs,
    gram_ss, gram_rs, grad_ss, grad_rs, relay_ss, relay_rs, pair_ss, pair_rs, fpart_ss, fpart_rs, fin_ss, fin_rs,
):
    e = lax.axis_index("expert")
    h = lax.axis_index("half")
    sub, width = tok_buf.shape[5:]
    hidden = wg.shape[1]
    tok = groups * sub
    rows = n * sub
    chips = n // 2
    columns = chips // 2
    parity = lax.rem(e, 2)
    chip = lax.div(e, 2)
    y = lax.rem(chip, 2)
    z = lax.div(chip, 2)
    sibling = e + 1 - 2 * parity
    other = 1 - h
    full = 2 * width

    def remote(src, dst, ssem, rsem, pe, ph):
        return pltpu.make_async_remote_copy(
            src_ref=src, dst_ref=dst, send_sem=ssem, recv_sem=rsem,
            device_id=(pe, ph), device_id_type=pl.DeviceIdType.MESH,
        )

    def send(*args):
        remote(*args).start()

    def flip(a, d):
        bit = 1
        out = a
        while bit <= d:
            if d & bit:
                out = out + bit * (1 - 2 * lax.rem(lax.div(a, bit), 2))
            bit *= 2
        return out

    def arrived(slot, rsem):
        remote(slot, slot, line_ss, rsem, sibling, h).wait_recv()

    def drained(sent, ssem):
        remote(sent, sent, ssem, twin_rs.at[0, 0], sibling, h).wait_send()

    moves = [(tok_hbm.at[pl.ds(g * sub, sub)], tok_buf.at[h, g, z, y, parity]) for g in range(groups)]
    moves += [(ids_hbm, ids_ref), (probs_hbm, probs_ref), (pad_hbm, pad_ref)]
    moves += [(up_hbm.at[pl.ds(g * sub, sub)], up_ref.at[g]) for g in range(groups)]
    moves += [(wg_hbm.at[0], wg), (wu_hbm.at[0], wu), (wd_hbm.at[0], wd)]
    loads = [pltpu.make_async_copy(src, dst, w_sem.at[i]) for i, (src, dst) in enumerate(moves)]
    for c in loads:
        c.start()

    near = list(range(1, chips))
    outer = near[::-1]

    barrier = pltpu.get_barrier_semaphore()
    for d in reversed(range(1, n)):
        pl.semaphore_signal(
            barrier, inc=1, device_id=(flip(e, d), h), device_id_type=pl.DeviceIdType.MESH
        )
    for pe in (e, 4 * z + 2 * (1 - y) + parity):
        pl.semaphore_signal(
            barrier, inc=1, device_id=(pe, other), device_id_type=pl.DeviceIdType.MESH
        )
    pl.semaphore_wait(barrier, n + 1)

    across = 4 * z + 2 * (1 - y) + parity

    def spread(g, zz):
        slot = tok_buf.at[h, g, zz, y, parity]
        send(slot, slot, quad_ss.at[2], quad_rs.at[g, 2], across, other)
        send(slot, slot, quad_ss.at[0], quad_rs.at[g, 0], across, h)
        send(slot, slot, quad_ss.at[1], quad_rs.at[g, 1], e, other)
        send(slot, slot, twin_ss, twin_rs.at[g, h], sibling, h)

    for g in range(groups):
        loads[g].wait()
        mine = tok_buf.at[h, g, z, y, parity]
        for dz in reversed(range(1, columns)):
            send(mine, mine, line_ss, line_rs.at[g, dz], 4 * flip(z, dz) + 2 * y + parity, h)
        spread(g, z)

    for c in loads[groups:-3]:
        c.wait()
    eye = (
        lax.broadcasted_iota(jnp.int32, (tok, tok), 0)
        == lax.broadcasted_iota(jnp.int32, (tok, tok), 1)
    )
    top = ids_ref.shape[0]
    lane = lax.broadcasted_iota(jnp.int32, (tok, top), 1)

    def column(row):
        return jnp.sum(jnp.where(eye, jnp.broadcast_to(row, (tok, tok)), 0.0), axis=1, keepdims=True)

    ids = jnp.zeros((tok, top), jnp.float32)
    probs = jnp.zeros((tok, top), jnp.float32)
    for j in range(top):
        ids = jnp.where(lane == j, column(ids_ref[j:j + 1, :].astype(jnp.float32)), ids)
        probs = jnp.where(lane == j, column(probs_ref[j:j + 1, :]), probs)
    pad = column(pad_ref[...].astype(jnp.float32))
    shares = probs / jnp.sum(probs, axis=1, keepdims=True)
    for i in range(n):
        share = jnp.sum(jnp.where(ids == float(i), shares, 0.0), axis=1, keepdims=True)
        for g in range(groups):
            share_s[g, i // 2, i % 2] = jnp.broadcast_to(
                share[g * sub:(g + 1) * sub], (sub, share_s.shape[4])
            )

    def lines(g):
        for dz in range(1, columns):
            zz = flip(z, dz)
            arrived(tok_buf.at[h, g, zz, y, parity], line_rs.at[g, dz])
            spread(g, zz)

    def gathered(g):
        for k, ph, yy in ((0, h, 1 - y), (1, other, y), (2, other, 1 - y)):
            slots = tok_buf.at[ph, g, :, yy, parity]
            arrived(slots, quad_rs.at[g, k])
            send(slots, slots, twin_ss, twin_rs.at[g, ph], sibling, h)

    def twins(g):
        for ph in range(2):
            arrived(tok_buf.at[ph, g, :, :, 0], twin_rs.at[g, ph])

    def hidden_rows(g):
        at = pl.ds(g * rows, rows)

        def hidden_step(cols, size):
            near_x = tok_buf[0, g].reshape(rows, width)
            far_x = tok_buf[1, g].reshape(rows, width)
            gate = dot(near_x, wg[:width, cols]) + dot(far_x, wg[width:, cols])
            up = dot(near_x, wu[:width, cols]) + dot(far_x, wu[width:, cols])
            gate_v[at, cols] = gate
            up_v[at, cols] = up
            hid[at, cols] = (gate / (1.0 + jnp.exp(-gate)) * up).astype(jnp.bfloat16)

        tiles(hidden, hidden_step)

    def down(g, far):
        start = (other if far else h) * width

        def down_step(cols, size):
            at = pl.ds(pl.multiple_of(cols.start + start, size), size)
            part = dot(hid[pl.ds(g * rows, rows), :], wd[:, at])
            osend[g, far, :, :, :, cols] = part.reshape(chips, 2, sub, size).astype(jnp.bfloat16)

        tiles(width, down_step, 1024)

    def cross_parts(g):
        for d in outer + [0]:
            pm = flip(chip, d)
            send(osend.at[g, 1, pm], orecv.at[g, pm], part_ss, part_rs.at[g, d], e, other)

    def forward(g, first, last):
        for d in (outer + [0])[first:last]:
            pm = flip(chip, d)
            arrived(orecv.at[g, pm], part_rs.at[g, d])
            total = osend[g, 0, pm].astype(jnp.float32) + orecv[g, pm].astype(jnp.float32)
            ored[g, pm] = total.astype(jnp.bfloat16)
            home = xrecv.at[g, chip, parity]
            if d:
                for q in range(2):
                    send(ored.at[g, pm, q], home, out_ss.at[0], out_rs.at[g, d], 2 * pm + q, h)
            else:
                send(ored.at[g, pm, 1 - parity], home, out_ss.at[1], out_rs.at[g, d], sibling, h)
                xrecv[g, chip, parity] = ored[g, chip, parity]

    same = (
        lax.rem(lax.broadcasted_iota(jnp.int32, (sub, rows), 1), sub)
        == lax.broadcasted_iota(jnp.int32, (sub, rows), 0)
    ).astype(jnp.float32)
    apart = (
        lax.div(lax.broadcasted_iota(jnp.int32, (n, rows), 1), sub)
        != lax.broadcasted_iota(jnp.int32, (n, rows), 0)
    ).astype(jnp.float32)

    def share_of(g, pm):
        return share_s[g, pm][:, :, :1]

    def products(g):
        layer = jnp.zeros((sub, width), jnp.float32)
        for d in [0] + near:
            pm = flip(chip, d)
            share = share_of(g, pm)
            arrived(xrecv.at[g, pm] if d else xrecv.at[g, chip, 1 - parity], out_rs.at[g, d])
            value = jnp.where(share > 0.0, xrecv[g, pm].astype(jnp.float32), 0.0)
            xs[g, pm] = value.astype(jnp.bfloat16)
            layer = layer + jnp.sum(share * value, axis=0)
        x_all = xs[g].reshape(rows, width)
        gram = dot_t(x_all, x_all).reshape(n, sub, rows) * same[None]
        gram_s[g, h] = jnp.sum(gram, axis=1)
        send(gram_s.at[g, h], gram_s.at[g, h], gram_ss, gram_rs.at[g], e, other)
        return layer

    def mix(g):
        arrived(gram_s.at[g, other], gram_rs.at[g])
        whole = (gram_s[g, 0] + gram_s[g, 1]) * (apart * (orth_weight / math.sqrt(full)))
        x_all = xs[g].reshape(rows, width)
        coeffs = (whole[:, None, :] * same[None]).reshape(rows, rows)
        high = coeffs.astype(jnp.bfloat16)
        low = (coeffs - high.astype(jnp.float32)).astype(jnp.bfloat16)
        mixed = (dot(high, x_all) + dot(low, x_all)).reshape(chips, 2, sub, width)
        upstream = up_ref[g].astype(jnp.float32)
        real = pad[g * sub:(g + 1) * sub]
        for i in range(chips):
            gsend[g, i] = (
                real[None] * (share_of(g, i) * upstream[None] + mixed[i])
            ).astype(jnp.bfloat16)
        slot = grows.at[h, g, chip, parity]
        send(gsend.at[g, chip, 1 - parity], slot, grad_ss.at[1], grad_rs.at[g, 0], sibling, h)
        send(gsend.at[g, chip, parity], slot, relay_ss, relay_rs.at[g], e, other)
        for d in near:
            pm = flip(chip, d)
            for q in range(2):
                send(gsend.at[g, pm, q], slot, grad_ss.at[0], grad_rs.at[g, d], 2 * pm + q, h)
        grows[h, g, chip, parity] = gsend[g, chip, parity]

    def relay(g, first, last):
        for d in range(first, last):
            slot = grows.at[h, g, flip(chip, d)] if d else grows.at[h, g, chip, 1 - parity]
            arrived(slot, grad_rs.at[g, d])
            send(slot, slot, relay_ss, relay_rs.at[g], e, other)

    def act(g, dh):
        ph = lax.rem(h + dh, 2)
        at = pl.ds(g * rows, rows)
        if dh:
            arrived(grows.at[other, g], relay_rs.at[g])

        def act_step(cols, size):
            depth = pl.ds(pl.multiple_of(ph * width, width), width)
            act = dot_t(grows[ph, g].reshape(rows, width), wd[cols, depth])
            if dh:
                act = act + act_v[at, cols]
                gate = gate_v[at, cols]
                sigma = 1.0 / (1.0 + jnp.exp(-gate))
                gg[at, cols] = (
                    act * up_v[at, cols] * sigma * (1.0 + gate * (1.0 - sigma))
                ).astype(jnp.bfloat16)
                gu[at, cols] = (act * gate * sigma).astype(jnp.bfloat16)
            else:
                act_v[at, cols] = act

        tiles(hidden, act_step)

    def back(g, far, piece, pieces):
        size = width // pieces
        start = (other if far else h) * width + piece * size
        rows_at = pl.ds(g * rows, rows)
        at = pl.ds(pl.multiple_of(start, size), size)
        part = dot_t(gg[rows_at, :], wg[at, :]) + dot_t(gu[rows_at, :], wu[at, :])
        part = part.astype(jnp.bfloat16).reshape(columns, 2, 2, sub, size)
        for q in range(2):
            psend[g, far, q, :, :, :, piece * size:(piece + 1) * size] = part[:, :, q]
        if piece == pieces - 1:
            send(
                psend.at[g, far, 1 - parity], prec.at[g, far],
                pair_ss, pair_rs.at[g, far], sibling, h,
            )

    def pairs(g):
        arrived(prec.at[g, 1], pair_rs.at[g, 1])
        for dz in reversed(range(columns)):
            zz = flip(z, dz)
            fsend[g, zz] = (
                psend[g, 1, parity, zz].astype(jnp.float32) + prec[g, 1, zz].astype(jnp.float32)
            ).astype(jnp.bfloat16)
            send(fsend.at[g, zz], frecv.at[g, zz], fpart_ss, fpart_rs.at[g, dz], e, other)

    def finish(g):
        arrived(prec.at[g, 0], pair_rs.at[g, 0])
        for dz in reversed(range(columns)):
            zz = flip(z, dz)
            total = psend[g, 0, parity, zz].astype(jnp.float32) + prec[g, 0, zz].astype(jnp.float32)
            arrived(frecv.at[g, zz], fpart_rs.at[g, dz])
            rsend[g, zz] = (total + frecv[g, zz].astype(jnp.float32)).astype(jnp.bfloat16)
            for dy in (1, 0):
                yy = flip(y, dy)
                if dz or dy:
                    send(
                        rsend.at[g, zz, yy], fin.at[g, chip],
                        fin_ss, fin_rs.at[g], 4 * zz + 2 * yy + parity, h,
                    )
                else:
                    fin[g, chip] = rsend[g, z, y]

    def collect(g):
        arrived(fin.at[g, pl.ds(0, chips - 1)], fin_rs.at[g])
        return jnp.sum(fin[g].astype(jnp.float32), axis=0)

    lines(0)
    lines(1)
    gathered(0)
    twins(0)
    for c in loads[-3:-1]:
        c.wait()
    hidden_rows(0)
    loads[-1].wait()
    down(0, 1)
    cross_parts(0)
    gathered(1)
    down(0, 0)
    twins(1)
    hidden_rows(1)
    forward(0, 0, chips // 4)
    down(1, 1)
    cross_parts(1)
    forward(0, chips // 4, chips)
    down(1, 0)
    forward(1, 0, 5 * chips // 8)
    layer_a = products(0)
    forward(1, 5 * chips // 8, chips)
    mix(0)
    layer_b = products(1)
    relay(0, 0, chips // 4)
    mix(1)
    layer_ref[...] = jnp.concatenate([layer_a, layer_b], axis=0).astype(jnp.bfloat16)
    relay(0, chips // 4, chips)
    act(0, 0)
    relay(1, 0, chips // 2)
    act(0, 1)
    relay(1, chips // 2, 5 * chips // 8)
    back(0, 1, 0, 2)
    relay(1, 5 * chips // 8, 6 * chips // 8)
    back(0, 1, 1, 2)
    relay(1, 6 * chips // 8, 7 * chips // 8)
    back(0, 0, 0, 2)
    relay(1, 7 * chips // 8, chips)
    back(0, 0, 1, 2)
    pairs(0)
    act(1, 0)
    act(1, 1)
    back(1, 1, 0, 1)
    back(1, 0, 0, 1)
    pairs(1)
    finish(0)
    finish(1)
    total_a = collect(0)
    total_b = collect(1)
    gtok_ref[...] = jnp.concatenate([total_a, total_b], axis=0).astype(jnp.bfloat16)
    drained(tok_buf.at[0, :, pl.ds(0, columns - 1), 0, 0], line_ss)
    for k in range(3):
        drained(tok_buf.at[0, :, :, 0, 0], quad_ss.at[k])
    drained(tok_buf.at[0], twin_ss)
    drained(osend.at[:, 1], part_ss)
    drained(ored.at[:, pl.ds(0, chips - 1)], out_ss.at[0])
    drained(ored.at[:, 0, 0], out_ss.at[1])
    drained(gram_s.at[:, 0], gram_ss)
    drained(gsend.at[:, pl.ds(0, chips - 1)], grad_ss.at[0])
    drained(gsend.at[:, 0, 0], grad_ss.at[1])
    drained(grows.at[0], relay_ss)
    drained(psend.at[:, :, 0], pair_ss)
    drained(fsend, fpart_ss)
    drained(fin.at[:, pl.ds(0, chips - 1)], fin_ss)


def fused(tokens, upstream, expert_ids, gate_probs, pad_mask, gate_weight, up_weight, down_weight):
    n, groups = lax.axis_size("expert"), 2
    tok, width = tokens.shape
    hidden = gate_weight.shape[2]
    sub, full, chips = tok // groups, 2 * width, n // 2
    columns, every = chips // 2, n * tok
    top = expert_ids.shape[1]
    low, wide = jnp.bfloat16, jnp.float32
    vmem, dma = pltpu.VMEM, pltpu.SemaphoreType.DMA
    local = pl.BlockSpec(memory_space=pltpu.VMEM)
    remain = pl.BlockSpec(memory_space=pl.ANY)
    outs = pl.pallas_call(
        functools.partial(fused_kernel, n, groups),
        out_shape=[vmem((tok, width), low)] * 2,
        in_specs=[remain] * 8,
        out_specs=[local] * 2,
        scratch_shapes=[
            vmem((groups, sub, width), low),
            vmem((top, tok), jnp.int32),
            vmem((top, tok), wide),
            vmem((1, tok), jnp.int32),
            vmem((2, groups, columns, 2, 2, sub, width), low),
            vmem((full, hidden), low),
            vmem((full, hidden), low),
            vmem((hidden, full), low),
            vmem((every, hidden), wide),
            vmem((every, hidden), wide),
            vmem((every, hidden), wide),
            vmem((every, hidden), low),
            vmem((every, hidden), low),
            vmem((every, hidden), low),
            vmem((groups, 2, chips, 2, sub, width), low),
            vmem((groups, chips, 2, sub, width), low),
            vmem((groups, chips, 2, sub, width), low),
            vmem((groups, chips, 2, sub, width), low),
            vmem((groups, chips, 2, sub, width), low),
            vmem((groups, 2, n, n * sub), wide),
            vmem((groups, chips, 2, sub, 128), wide),
            vmem((groups, chips, 2, sub, width), low),
            vmem((2, groups, chips, 2, sub, width), low),
            vmem((groups, 2, 2, columns, 2, sub, width), low),
            vmem((groups, 2, columns, 2, sub, width), low),
            vmem((groups, columns, 2, sub, width), low),
            vmem((groups, columns, 2, sub, width), low),
            vmem((groups, columns, 2, sub, width), low),
            vmem((groups, chips, sub, width), low),
            dma((2 * groups + 6,)),
            dma(()),
            dma((3,)),
            dma(()),
            dma((groups, columns)),
            dma((groups, 3)),
            dma((groups, 2)),
            dma(()),
            dma((groups, chips)),
            dma((2,)),
            dma((groups, chips)),
            dma(()),
            dma((groups,)),
            dma((2,)),
            dma((groups, chips)),
            dma(()),
            dma((groups,)),
            dma(()),
            dma((groups, 2)),
            dma(()),
            dma((groups, columns)),
            dma(()),
            dma((groups,)),
        ],
        compiler_params=pltpu.CompilerParams(
            collective_id=0, has_side_effects=True, vmem_limit_bytes=56 * 1024 * 1024
        ),
        name="experts",
    )(
        tokens, upstream, expert_ids.T, gate_probs.T, pad_mask.reshape(1, tok),
        gate_weight, up_weight, down_weight,
    )
    result = [jax.ShapeDtypeStruct((tok, width), low)] * 2
    return pl.pallas_call(
        copy_kernel, out_shape=result, in_specs=[local] * 2, out_specs=[local] * 2, name="results"
    )(*[pltpu.with_memory_space_constraint(out, pltpu.VMEM) for out in outs])


def shards(tokens, upstream, expert_ids, gate_probs, pad_mask, gate_weight, up_weight, down_weight):
    tok_count, top_count = expert_ids.shape
    experts = lax.axis_size("expert")
    capacity = min(tok_count, 2 * tok_count * top_count // experts)
    paired = experts > 3 and experts & (experts - 1) == 0 and lax.axis_size("half") == 2
    if capacity == tok_count and tok_count % 16 == 0 and paired:
        return fused(
            tokens, upstream, expert_ids, gate_probs, pad_mask, gate_weight, up_weight, down_weight
        )
    slots_total = experts * capacity
    full_width = tokens.shape[1] * lax.axis_size("half")
    slot_dest = assign_slots(expert_ids, experts, capacity)
    place_items = placement_matrix(slot_dest, slots_total)
    place_tokens = jnp.sum(place_items.reshape(slots_total, tok_count, top_count), axis=2)
    weight_gate = gate_weight[0]
    weight_up = up_weight[0]
    weight_down = down_weight[0]
    rows_in = to_experts(place_tokens, tokens)
    gate_val = jnp.dot(rows_in, weight_gate, preferred_element_type=jnp.float32)
    up_val = jnp.dot(rows_in, weight_up, preferred_element_type=jnp.float32)
    hidden_act = (jax.nn.silu(gate_val) * up_val).astype(jnp.bfloat16)
    partial_value = jnp.dot(hidden_act, weight_down, preferred_element_type=jnp.float32)
    out_home = to_homes(partial_value)
    outputs = jnp.take(out_home, slot_dest, axis=0).reshape(tok_count, top_count, -1)
    out_float = outputs.astype(jnp.float32)
    shares = gate_probs / jnp.sum(gate_probs, axis=1, keepdims=True)
    layer_out = jnp.sum(shares[:, :, None] * out_float, axis=1).astype(jnp.bfloat16)
    gram_part = jnp.einsum("tjd,tkd->tjk", out_float, out_float) / math.sqrt(full_width)
    gram = lax.psum(gram_part, "half")
    off_diag = 1.0 - jnp.eye(top_count, dtype=jnp.float32)
    coeffs = orth_weight * gram * off_diag
    grad_out = pad_mask.astype(jnp.float32)[:, None, None] * (
        shares[:, :, None] * upstream.astype(jnp.float32)[:, None, :]
        + jnp.einsum("tjk,tkd->tjd", coeffs, out_float)
    )
    grad_items = grad_out.astype(jnp.bfloat16).reshape(tok_count * top_count, -1)
    grad_rows = to_experts(place_items, grad_items)
    grad_act = jnp.einsum("rd,hd->rh", grad_rows, weight_down, preferred_element_type=jnp.float32)
    sigma = jax.nn.sigmoid(gate_val)
    grad_gate = (grad_act * up_val * sigma * (1.0 + gate_val * (1.0 - sigma))).astype(jnp.bfloat16)
    grad_up = (grad_act * gate_val * sigma).astype(jnp.bfloat16)
    grad_partial = jnp.einsum(
        "rh,dh->rd", grad_gate, weight_gate, preferred_element_type=jnp.float32
    )
    grad_partial = grad_partial + jnp.einsum(
        "rh,dh->rd", grad_up, weight_up, preferred_element_type=jnp.float32
    )
    grad_home = to_homes(grad_partial)
    grad_pairs = jnp.take(grad_home, slot_dest, axis=0).reshape(tok_count, top_count, -1)
    grad_tokens = jnp.sum(grad_pairs.astype(jnp.float32), axis=1).astype(jnp.bfloat16)
    return (layer_out, grad_tokens)


def solution(mesh):
    in_specs = (
        P("expert", "half"),
        P("expert", "half"),
        P("expert", None),
        P("expert", None),
        P("expert"),
        P("expert", None, "half"),
        P("expert", None, "half"),
        P("expert", "half", None),
    )
    out_specs = (P("expert", "half"), P("expert", "half"))
    return jax.shard_map(shards, mesh=mesh, in_specs=in_specs, out_specs=out_specs, check_vma=False)
```

time: 75 us -> 64.7 us (0.86)
  Pallas kernels: 74.2 us -> 63.9 us
    pallas_call x1, Pallas kernels: 72.8 us -> 63.2 us  [fused(): pl.pallas_call(functools.partial(fused_kernel, n, groups), out_shape=[vme...]
    pallas_call x1, Pallas kernels: 1.4 us -> 0.63 us  [fused(): pl.pallas_call(copy_kernel, out_shape=result, in_specs=[local] * 2, out_s...]
where the time goes in v3:
time: 64.7 us; the launch traced here: 64.5 us
  Pallas kernels  63.9 us (99%)
    pallas_call x1, Pallas kernels, fused(): pl.pallas_call(functools.partial(fused_kernel, n, groups), out_shape=[vme...  63.2 us

profile of v3, /device:TPU:0, one launch (start us, length us, event | category | flops | bytes accessed | tf_op | source)
XLA Modules:
  0.0 64.5 jit_solution(16736994755104109378)
XLA Ops:
  0.6 63.2 %experts.1 = (bf16[16,1024]{1,0:T(8,128)(2,1)S(1)}, bf16[16,1024]{1,0:T(8,128)(2,1)S(1)}) custom-call(bf16[16,1024]{1,0:T(8,128)(2,1)} %tok_hbm.1, bf16[16,1024]{1,0:T(8,128)(2,1)} %up_hbm.1, s32[8,16]{1,0:T(8,128)} %bitcast.3, f32[8,16]{1,0:T(8,128)} %bitcast.4, s32[1,16]{1,0:T(1,128)} %bitcast.5, bf16[1,2048,768]{2,1,0:T(8,128)(2,1)} %wg_hbm.1, ...), custom_call_target="tpu_custom_call" | custom-call | tf_op jit(solution)/shard_map/experts/pallas_call | solution.py:441
  63.9 0.6 results.1

commit v4 on v3

--- a/solution.py
+++ b/solution.py
@@ -39,7 +39,7 @@
 
 
 def block_of(width, most):
-    return next((b for b in (1024, 512, 256, 128) if b <= most and width % b == 0), width)
+    return next((b for b in (1024, 512, 384, 256, 128) if b <= most and width % b == 0), width)
 
 
 def tiles(width, body, most=256):
@@ -71,9 +71,11 @@
     layer_ref, gtok_ref,
     up_ref, ids_ref, probs_ref, pad_ref,
     tok_buf, wg, wu, wd, gate_v, up_v, act_v, hid, gg, gu,
-    osend, orecv, ored, xrecv, xs, gram_s, share_s, gsend, grows, psend, prec, fsend, frecv, rsend, fin,
+    wg_t, wu_t, wd_t,
+    osend, orecv, ored, xrecv, xs, gram_s, share_s, gsend, grows, psend, prec,
+    lsend, lrecv, lsum, lfin, rsend, rrecv, rsum, rfin,
     w_sem, line_ss, quad_ss, twin_ss, line_rs, quad_rs, twin_rs, part_ss, part_rs, out_ss, out_rs,
-    gram_ss, gram_rs, grad_ss, grad_rs, relay_ss, relay_rs, pair_ss, pair_rs, fpart_ss, fpart_rs, fin_ss, fin_rs,
+    gram_ss, gram_rs, grad_ss, grad_rs, relay_ss, relay_rs, pair_ss, pair_rs, lpart_ss, lpart_rs, rpart_ss, rpart_rs, fin_ss, fin_rs,
 ):
     e = lax.axis_index("expert")
     h = lax.axis_index("half")
@@ -90,6 +92,12 @@
     sibling = e + 1 - 2 * parity
     other = 1 - h
     full = 2 * width
+    half_width = width // 2
+    block = columns // 2
+    own_block = lax.div(z, block)
+
+    def blocks(far):
+        return pl.ds((1 - own_block if far else own_block) * block, block)
 
     def remote(src, dst, ssem, rsem, pe, ph):
         return pltpu.make_async_remote_copy(
@@ -139,11 +147,12 @@
 
     across = 4 * z + 2 * (1 - y) + parity
 
-    def spread(g, zz):
-        slot = tok_buf.at[h, g, zz, y, parity]
-        send(slot, slot, quad_ss.at[2], quad_rs.at[g, 2], across, other)
-        send(slot, slot, quad_ss.at[0], quad_rs.at[g, 0], across, h)
-        send(slot, slot, quad_ss.at[1], quad_rs.at[g, 1], e, other)
+    def spread(g, dz):
+        slot = tok_buf.at[h, g, flip(z, dz), y, parity]
+        k = dz // block
+        send(slot, slot, quad_ss.at[2], quad_rs.at[g, 2, k], across, other)
+        send(slot, slot, quad_ss.at[0], quad_rs.at[g, 0, k], across, h)
+        send(slot, slot, quad_ss.at[1], quad_rs.at[g, 1, k], e, other)
         send(slot, slot, twin_ss, twin_rs.at[g, h], sibling, h)
 
     for g in range(groups):
@@ -151,7 +160,7 @@
         mine = tok_buf.at[h, g, z, y, parity]
         for dz in reversed(range(1, columns)):
             send(mine, mine, line_ss, line_rs.at[g, dz], 4 * flip(z, dz) + 2 * y + parity, h)
-        spread(g, z)
+        spread(g, 0)
 
     for c in loads[groups:-3]:
         c.wait()
@@ -183,22 +192,24 @@
         for dz in range(1, columns):
             zz = flip(z, dz)
             arrived(tok_buf.at[h, g, zz, y, parity], line_rs.at[g, dz])
-            spread(g, zz)
+            spread(g, dz)
 
     def gathered(g):
-        for k, ph, yy in ((0, h, 1 - y), (1, other, y), (2, other, 1 - y)):
-            slots = tok_buf.at[ph, g, :, yy, parity]
-            arrived(slots, quad_rs.at[g, k])
-            send(slots, slots, twin_ss, twin_rs.at[g, ph], sibling, h)
+        for far in range(2):
+            for k, ph, yy in ((0, h, 1 - y), (1, other, y), (2, other, 1 - y)):
+                slots = tok_buf.at[ph, g, blocks(far), yy, parity]
+                arrived(slots, quad_rs.at[g, k, far])
+                send(slots, slots, twin_ss, twin_rs.at[g, ph], sibling, h)
 
     def twins(g):
         for ph in range(2):
             arrived(tok_buf.at[ph, g, :, :, 0], twin_rs.at[g, ph])
 
-    def hidden_rows(g):
+    def hidden_rows(g, first, last):
         at = pl.ds(g * rows, rows)
-
-        def hidden_step(cols, size):
+        size = block_of(hidden, 256)
+
+        def hidden_step(cols):
             near_x = tok_buf[0, g].reshape(rows, width)
             far_x = tok_buf[1, g].reshape(rows, width)
             gate = dot(near_x, wg[:width, cols]) + dot(far_x, wg[width:, cols])
@@ -207,7 +218,9 @@
             up_v[at, cols] = up
             hid[at, cols] = (gate / (1.0 + jnp.exp(-gate)) * up).astype(jnp.bfloat16)
 
-        tiles(hidden, hidden_step)
+        count = hidden // size
+        for i in range(first * count // 3, last * count // 3):
+            hidden_step(slice(i * size, (i + 1) * size))
 
     def down(g, far):
         start = (other if far else h) * width
@@ -302,7 +315,7 @@
 
         def act_step(cols, size):
             depth = pl.ds(pl.multiple_of(ph * width, width), width)
-            act = dot_t(grows[ph, g].reshape(rows, width), wd[cols, depth])
+            act = dot(grows[ph, g].reshape(rows, width), wd_t[depth, cols])
             if dh:
                 act = act + act_v[at, cols]
                 gate = gate_v[at, cols]
@@ -314,52 +327,102 @@
             else:
                 act_v[at, cols] = act
 
-        tiles(hidden, act_step)
-
-    def back(g, far, piece, pieces):
-        size = width // pieces
-        start = (other if far else h) * width + piece * size
+        tiles(hidden, act_step, 384)
+
+    def turn(first, last):
+        for i in range(first, last):
+            at = slice((i // 3) * half_width, (i // 3 + 1) * half_width)
+            if i % 3 == 0:
+                wd_t[at, :] = wd[:, at].T
+            elif i % 3 == 1:
+                wg_t[:, at] = wg[at, :].T
+            else:
+                wu_t[:, at] = wu[at, :].T
+
+    def back(g, far):
         rows_at = pl.ds(g * rows, rows)
-        at = pl.ds(pl.multiple_of(start, size), size)
-        part = dot_t(gg[rows_at, :], wg[at, :]) + dot_t(gu[rows_at, :], wu[at, :])
-        part = part.astype(jnp.bfloat16).reshape(columns, 2, 2, sub, size)
+        at = pl.ds(pl.multiple_of((other if far else h) * width, width), width)
+        part = dot(gg[rows_at, :], wg_t[:, at]) + dot(gu[rows_at, :], wu_t[:, at])
+        part = part.astype(jnp.bfloat16).reshape(columns, 2, 2, sub, width)
         for q in range(2):
-            psend[g, far, q, :, :, :, piece * size:(piece + 1) * size] = part[:, :, q]
-        if piece == pieces - 1:
-            send(
-                psend.at[g, far, 1 - parity], prec.at[g, far],
-                pair_ss, pair_rs.at[g, far], sibling, h,
-            )
+            psend[g, far, q] = part[:, :, q]
+        send(
+            psend.at[g, far, 1 - parity], prec.at[g, far],
+            pair_ss, pair_rs.at[g, far], sibling, h,
+        )
+
+    left, right = slice(0, half_width), slice(half_width, width)
 
     def pairs(g):
         arrived(prec.at[g, 1], pair_rs.at[g, 1])
         for dz in reversed(range(columns)):
             zz = flip(z, dz)
-            fsend[g, zz] = (
-                psend[g, 1, parity, zz].astype(jnp.float32) + prec[g, 1, zz].astype(jnp.float32)
+            lsend[g, zz] = (
+                psend[g, 1, parity, zz, :, :, left].astype(jnp.float32)
+                + prec[g, 1, zz, :, :, left].astype(jnp.float32)
             ).astype(jnp.bfloat16)
-            send(fsend.at[g, zz], frecv.at[g, zz], fpart_ss, fpart_rs.at[g, dz], e, other)
+            send(lsend.at[g, zz], lrecv.at[g, zz], lpart_ss, lpart_rs.at[g, dz], e, other)
+        for far in (1, 0):
+            if not far:
+                arrived(prec.at[g, 0], pair_rs.at[g, 0])
+            for k in (1, 0):
+                zs = blocks(k)
+                rsend[g, far, zs] = (
+                    psend[g, far, parity, zs, 1 - y, :, right].astype(jnp.float32)
+                    + prec[g, far, zs, 1 - y, :, right].astype(jnp.float32)
+                ).astype(jnp.bfloat16)
+                send(
+                    rsend.at[g, far, zs], rrecv.at[g, far, zs],
+                    rpart_ss, rpart_rs.at[g, far, k], across, h,
+                )
+
+    def finish_left(g, dz):
+        zz = flip(z, dz)
+        total = (
+            psend[g, 0, parity, zz, :, :, left].astype(jnp.float32)
+            + prec[g, 0, zz, :, :, left].astype(jnp.float32)
+        )
+        arrived(lrecv.at[g, zz], lpart_rs.at[g, dz])
+        lsum[g, zz] = (total + lrecv[g, zz].astype(jnp.float32)).astype(jnp.bfloat16)
+        for dy in (1, 0):
+            yy = flip(y, dy)
+            if dz or dy:
+                send(
+                    lsum.at[g, zz, yy], lfin.at[g, chip],
+                    fin_ss.at[0], fin_rs.at[g, 0], 4 * zz + 2 * yy + parity, h,
+                )
+            else:
+                lfin[g, chip] = lsum[g, z, y]
+
+    def finish_right(g, far, k):
+        zs = blocks(k)
+        total = (
+            psend[g, far, parity, zs, y, :, right].astype(jnp.float32)
+            + prec[g, far, zs, y, :, right].astype(jnp.float32)
+        )
+        arrived(rrecv.at[g, far, zs], rpart_rs.at[g, far, k])
+        rsum[g, far, zs] = (total + rrecv[g, far, zs].astype(jnp.float32)).astype(jnp.bfloat16)
+        for dz in reversed(range(k * block, (k + 1) * block)):
+            zz = flip(z, dz)
+            if dz or far:
+                send(
+                    rsum.at[g, far, zz], rfin.at[g, columns * h + z],
+                    fin_ss.at[1], fin_rs.at[g, 1], 4 * zz + 2 * y + parity, other if far else h,
+                )
+            else:
+                rfin[g, columns * h + z] = rsum[g, far, z]
 
     def finish(g):
-        arrived(prec.at[g, 0], pair_rs.at[g, 0])
-        for dz in reversed(range(columns)):
-            zz = flip(z, dz)
-            total = psend[g, 0, parity, zz].astype(jnp.float32) + prec[g, 0, zz].astype(jnp.float32)
-            arrived(frecv.at[g, zz], fpart_rs.at[g, dz])
-            rsend[g, zz] = (total + frecv[g, zz].astype(jnp.float32)).astype(jnp.bfloat16)
-            for dy in (1, 0):
-                yy = flip(y, dy)
-                if dz or dy:
-                    send(
-                        rsend.at[g, zz, yy], fin.at[g, chip],
-                        fin_ss, fin_rs.at[g], 4 * zz + 2 * yy + parity, h,
-                    )
-                else:
-                    fin[g, chip] = rsend[g, z, y]
+        for k in (1, 0):
+            for far in (1, 0):
+                for dz in reversed(range((2 * k + far) * block // 2, (2 * k + far + 1) * block // 2)):
+                    finish_left(g, dz)
+                finish_right(g, far, k)
 
     def collect(g):
-        arrived(fin.at[g, pl.ds(0, chips - 1)], fin_rs.at[g])
-        return jnp.sum(fin[g].astype(jnp.float32), axis=0)
+        arrived(lfin.at[g, pl.ds(0, chips - 1)], fin_rs.at[g, 0])
+        arrived(rfin.at[g, pl.ds(0, chips - 1)], fin_rs.at[g, 1])
+        return [jnp.sum(fin[g].astype(jnp.float32), axis=0) for fin in (lfin, rfin)]
 
     lines(0)
     lines(1)
@@ -367,50 +430,69 @@
     twins(0)
     for c in loads[-3:-1]:
         c.wait()
-    hidden_rows(0)
+    hidden_rows(0, 0, 3)
     loads[-1].wait()
     down(0, 1)
     cross_parts(0)
     gathered(1)
     down(0, 0)
     twins(1)
-    hidden_rows(1)
-    forward(0, 0, chips // 4)
+    hidden_rows(1, 0, 2)
+    forward(0, 0, chips // 8)
+    hidden_rows(1, 2, 3)
+    forward(0, chips // 8, 3 * chips // 8)
     down(1, 1)
     cross_parts(1)
-    forward(0, chips // 4, chips)
+    turn(0, 1)
+    forward(0, 3 * chips // 8, chips // 2)
+    turn(1, 2)
+    forward(0, chips // 2, 5 * chips // 8)
+    turn(2, 3)
+    forward(0, 5 * chips // 8, 3 * chips // 4)
+    turn(3, 4)
+    forward(0, 3 * chips // 4, 7 * chips // 8)
+    turn(4, 5)
+    forward(0, 7 * chips // 8, chips)
     down(1, 0)
-    forward(1, 0, 5 * chips // 8)
+    forward(1, 0, chips // 8)
+    turn(5, 6)
+    forward(1, chips // 8, chips // 4)
+    turn(6, 7)
+    forward(1, chips // 4, 3 * chips // 8)
+    turn(7, 8)
+    forward(1, 3 * chips // 8, chips // 2)
+    turn(8, 9)
+    forward(1, chips // 2, 5 * chips // 8)
+    turn(9, 10)
     layer_a = products(0)
     forward(1, 5 * chips // 8, chips)
+    turn(10, 12)
     mix(0)
     layer_b = products(1)
-    relay(0, 0, chips // 4)
+    relay(0, 0, 3 * chips // 8)
     mix(1)
     layer_ref[...] = jnp.concatenate([layer_a, layer_b], axis=0).astype(jnp.bfloat16)
-    relay(0, chips // 4, chips)
+    relay(0, 3 * chips // 8, chips)
     act(0, 0)
-    relay(1, 0, chips // 2)
+    relay(1, 0, 5 * chips // 8)
     act(0, 1)
-    relay(1, chips // 2, 5 * chips // 8)
-    back(0, 1, 0, 2)
     relay(1, 5 * chips // 8, 6 * chips // 8)
-    back(0, 1, 1, 2)
+    back(0, 1)
     relay(1, 6 * chips // 8, 7 * chips // 8)
-    back(0, 0, 0, 2)
+    back(0, 0)
     relay(1, 7 * chips // 8, chips)
-    back(0, 0, 1, 2)
+    act(1, 0)
     pairs(0)
-    act(1, 0)
     act(1, 1)
-    back(1, 1, 0, 1)
-    back(1, 0, 0, 1)
+    back(1, 1)
+    back(1, 0)
+    finish(0)
     pairs(1)
-    finish(0)
     finish(1)
     total_a = collect(0)
     total_b = collect(1)
-    gtok_ref[...] = jnp.concatenate([total_a, total_b], axis=0).astype(jnp.bfloat16)
+    for k, at in enumerate((left, right)):
+        gtok_ref[:, at] = jnp.concatenate([total_a[k], total_b[k]], axis=0).astype(jnp.bfloat16)
     drained(tok_buf.at[0, :, pl.ds(0, columns - 1), 0, 0], line_ss)
     for k in range(3):
         drained(tok_buf.at[0, :, :, 0, 0], quad_ss.at[k])
@@ -423,8 +505,10 @@
     drained(gsend.at[:, 0, 0], grad_ss.at[1])
     drained(grows.at[0], relay_ss)
     drained(psend.at[:, :, 0], pair_ss)
-    drained(fsend, fpart_ss)
-    drained(fin.at[:, pl.ds(0, chips - 1)], fin_ss)
+    drained(lsend, lpart_ss)
+    drained(rsend, rpart_ss)
+    drained(lfin.at[:, pl.ds(0, chips - 1)], fin_ss.at[0])
+    drained(rfin.at[:, pl.ds(0, chips - 1)], fin_ss.at[1])
 
 
 def fused(tokens, upstream, expert_ids, gate_probs, pad_mask, gate_weight, up_weight, down_weight):
@@ -458,6 +542,9 @@
             vmem((every, hidden), low),
             vmem((every, hidden), low),
             vmem((every, hidden), low),
+            vmem((hidden, full), low),
+            vmem((hidden, full), low),
+            vmem((full, hidden), low),
             vmem((groups, 2, chips, 2, sub, width), low),
             vmem((groups, chips, 2, sub, width), low),
             vmem((groups, chips, 2, sub, width), low),
@@ -469,16 +556,20 @@
             vmem((2, groups, chips, 2, sub, width), low),
             vmem((groups, 2, 2, columns, 2, sub, width), low),
             vmem((groups, 2, columns, 2, sub, width), low),
-            vmem((groups, columns, 2, sub, width), low),
-            vmem((groups, columns, 2, sub, width), low),
-            vmem((groups, columns, 2, sub, width), low),
-            vmem((groups, chips, sub, width), low),
+            vmem((groups, columns, 2, sub, width // 2), low),
+            vmem((groups, columns, 2, sub, width // 2), low),
+            vmem((groups, columns, 2, sub, width // 2), low),
+            vmem((groups, chips, sub, width // 2), low),
+            vmem((groups, 2, columns, sub, width // 2), low),
+            vmem((groups, 2, columns, sub, width // 2), low),
+            vmem((groups, 2, columns, sub, width // 2), low),
+            vmem((groups, chips, sub, width // 2), low),
             dma((2 * groups + 6,)),
             dma(()),
             dma((3,)),
             dma(()),
             dma((groups, columns)),
-            dma((groups, 3)),
+            dma((groups, 3, 2)),
             dma((groups, 2)),
             dma(()),
             dma((groups, chips)),
@@ -495,7 +586,9 @@
             dma(()),
             dma((groups, columns)),
             dma(()),
-            dma((groups,)),
+            dma((groups, 2, 2)),
+            dma((2,)),
+            dma((groups, 2)),
         ],
         compiler_params=pltpu.CompilerParams(
             collective_id=0, has_side_effects=True, vmem_limit_bytes=56 * 1024 * 1024
@@ -515,7 +608,7 @@
     tok_count, top_count = expert_ids.shape
     experts = lax.axis_size("expert")
     capacity = min(tok_count, 2 * tok_count * top_count // experts)
-    paired = experts > 3 and experts & (experts - 1) == 0 and lax.axis_size("half") == 2
+    paired = experts > 15 and experts & (experts - 1) == 0 and lax.axis_size("half") == 2
     if capacity == tok_count and tok_count % 16 == 0 and paired:
         return fused(
             tokens, upstream, expert_ids, gate_probs, pad_mask, gate_weight, up_weight, down_weight

time: 64.7 us -> 61.3 us (0.947)
  Pallas kernels: 63.9 us -> 60.5 us
    pallas_call x1, Pallas kernels: 63.2 us -> 59.9 us  [fused(): pl.pallas_call(functools.partial(fused_kernel, n, groups), out_shape=[vme...]
where the time goes in v4:
time: 61.3 us; the launch traced here: 61.1 us
  Pallas kernels  60.5 us (99%)
  between operations  0.64 us (1%)
    pallas_call x1, Pallas kernels, fused(): pl.pallas_call(functools.partial(fused_kernel, n, groups), out_shape=[vme...  59.9 us

profile of v4, /device:TPU:0, one launch (start us, length us, event | category | flops | bytes accessed | tf_op | source)
XLA Modules:
  0.0 61.1 jit_solution(2251005115252622323)
XLA Ops:
  0.6 59.9 %experts.1 = (bf16[16,1024]{1,0:T(8,128)(2,1)S(1)}, bf16[16,1024]{1,0:T(8,128)(2,1)S(1)}) custom-call(bf16[16,1024]{1,0:T(8,128)(2,1)} %tok_hbm.1, bf16[16,1024]{1,0:T(8,128)(2,1)} %up_hbm.1, s32[8,16]{1,0:T(8,128)} %bitcast.3, f32[8,16]{1,0:T(8,128)} %bitcast.4, s32[1,16]{1,0:T(1,128)} %bitcast.5, bf16[1,2048,768]{2,1,0:T(8,128)(2,1)} %wg_hbm.1, ...), custom_call_target="tpu_custom_call" | custom-call | tf_op jit(solution)/shard_map/experts/pallas_call | solution.py:525
  60.5 0.6 %results.1 = (bf16[16,1024]{1,0:T(8,128)(2,1)}, bf16[16,1024]{1,0:T(8,128)(2,1)}) custom-call(bf16[16,1024]{1,0:T(8,128)(2,1)S(1)} %get-tuple-element.4.a_ref, bf16[16,1024]{1,0:T(8,128)(2,1)S(1)} %get-tuple-element.5.b_ref), custom_call_target="tpu_custom_call" | custom-call | tf_op jit(solution)/shard_map/results/pallas_call | solution.py:602

commit v5 on v4

--- a/solution.py
+++ b/solution.py
@@ -201,26 +201,31 @@
                 arrived(slots, quad_rs.at[g, k, far])
                 send(slots, slots, twin_ss, twin_rs.at[g, ph], sibling, h)
 
-    def twins(g):
-        for ph in range(2):
-            arrived(tok_buf.at[ph, g, :, :, 0], twin_rs.at[g, ph])
+    def twins(g, ph):
+        arrived(tok_buf.at[ph, g, :, :, 0], twin_rs.at[g, ph])
+
+    def column_tiles(size):
+        return [slice(i, i + size) for i in range(0, hidden, size)]
+
+    def own_rows(g):
+        at = pl.ds(g * rows, rows)
+        depth = pl.ds(pl.multiple_of(h * width, width), width)
+        for cols in column_tiles(block_of(hidden, 256)):
+            x = tok_buf[h, g].reshape(rows, width)
+            gate_v[at, cols] = dot(x, wg[depth, cols])
+            up_v[at, cols] = dot(x, wu[depth, cols])
 
     def hidden_rows(g, first, last):
         at = pl.ds(g * rows, rows)
-        size = block_of(hidden, 256)
-
-        def hidden_step(cols):
-            near_x = tok_buf[0, g].reshape(rows, width)
-            far_x = tok_buf[1, g].reshape(rows, width)
-            gate = dot(near_x, wg[:width, cols]) + dot(far_x, wg[width:, cols])
-            up = dot(near_x, wu[:width, cols]) + dot(far_x, wu[width:, cols])
+        depth = pl.ds(pl.multiple_of(other * width, width), width)
+        every = column_tiles(block_of(hidden, 256))
+        for cols in every[first * len(every) // 3:last * len(every) // 3]:
+            x = tok_buf[other, g].reshape(rows, width)
+            gate = gate_v[at, cols] + dot(x, wg[depth, cols])
+            up = up_v[at, cols] + dot(x, wu[depth, cols])
             gate_v[at, cols] = gate
             up_v[at, cols] = up
             hid[at, cols] = (gate / (1.0 + jnp.exp(-gate)) * up).astype(jnp.bfloat16)
-
-        count = hidden // size
-        for i in range(first * count // 3, last * count // 3):
-            hidden_step(slice(i * size, (i + 1) * size))
 
     def down(g, far):
         start = (other if far else h) * width
@@ -283,9 +288,7 @@
         whole = (gram_s[g, 0] + gram_s[g, 1]) * (apart * (orth_weight / math.sqrt(full)))
         x_all = xs[g].reshape(rows, width)
         coeffs = (whole[:, None, :] * same[None]).reshape(rows, rows)
-        high = coeffs.astype(jnp.bfloat16)
-        low = (coeffs - high.astype(jnp.float32)).astype(jnp.bfloat16)
-        mixed = (dot(high, x_all) + dot(low, x_all)).reshape(chips, 2, sub, width)
+        mixed = dot(coeffs.astype(jnp.bfloat16), x_all).reshape(chips, 2, sub, width)
         upstream = up_ref[g].astype(jnp.float32)
         real = pad[g * sub:(g + 1) * sub]
         for i in range(chips):
@@ -313,21 +316,19 @@
         if dh:
             arrived(grows.at[other, g], relay_rs.at[g])
 
-        def act_step(cols, size):
-            depth = pl.ds(pl.multiple_of(ph * width, width), width)
-            act = dot(grows[ph, g].reshape(rows, width), wd_t[depth, cols])
+        depth = pl.ds(pl.multiple_of(ph * width, width), width)
+        for cols in column_tiles(block_of(hidden, 384)):
+            part = dot(grows[ph, g].reshape(rows, width), wd_t[depth, cols])
             if dh:
-                act = act + act_v[at, cols]
+                part = part + act_v[at, cols]
                 gate = gate_v[at, cols]
                 sigma = 1.0 / (1.0 + jnp.exp(-gate))
                 gg[at, cols] = (
-                    act * up_v[at, cols] * sigma * (1.0 + gate * (1.0 - sigma))
+                    part * up_v[at, cols] * sigma * (1.0 + gate * (1.0 - sigma))
                 ).astype(jnp.bfloat16)
-                gu[at, cols] = (act * gate * sigma).astype(jnp.bfloat16)
+                gu[at, cols] = (part * gate * sigma).astype(jnp.bfloat16)
             else:
-                act_v[at, cols] = act
-
-        tiles(hidden, act_step, 384)
+                act_v[at, cols] = part
 
     def turn(first, last):
         for i in range(first, last):
@@ -427,16 +428,20 @@
     lines(0)
     lines(1)
     gathered(0)
-    twins(0)
+    twins(0, h)
     for c in loads[-3:-1]:
         c.wait()
+    own_rows(0)
+    twins(0, other)
     hidden_rows(0, 0, 3)
     loads[-1].wait()
     down(0, 1)
     cross_parts(0)
     gathered(1)
     down(0, 0)
-    twins(1)
+    twins(1, h)
+    own_rows(1)
+    twins(1, other)
     hidden_rows(1, 0, 2)
     forward(0, 0, chips // 8)
     hidden_rows(1, 2, 3)
@@ -462,25 +467,22 @@
     turn(7, 8)
     forward(1, 3 * chips // 8, chips // 2)
     turn(8, 9)
-    forward(1, chips // 2, 5 * chips // 8)
-    turn(9, 10)
     layer_a = products(0)
-    forward(1, 5 * chips // 8, chips)
-    turn(10, 12)
+    forward(1, chips // 2, chips)
+    turn(9, 12)
     mix(0)
     layer_b = products(1)
     relay(0, 0, 3 * chips // 8)
     mix(1)
     layer_ref[...] = jnp.concatenate([layer_a, layer_b], axis=0).astype(jnp.bfloat16)
     relay(0, 3 * chips // 8, chips)
+    relay(1, 0, 5 * chips // 8)
     act(0, 0)
-    relay(1, 0, 5 * chips // 8)
+    relay(1, 5 * chips // 8, 6 * chips // 8)
     act(0, 1)
-    relay(1, 5 * chips // 8, 6 * chips // 8)
+    relay(1, 6 * chips // 8, chips)
     back(0, 1)
-    relay(1, 6 * chips // 8, 7 * chips // 8)
     back(0, 0)
-    relay(1, 7 * chips // 8, chips)
     act(1, 0)
     pairs(0)
     act(1, 1)

time: 61.3 us -> 59.8 us (0.976)
  Pallas kernels: 60.5 us -> 59 us
    pallas_call x1, Pallas kernels: 59.9 us -> 58.4 us  [fused(): pl.pallas_call(functools.partial(fused_kernel, n, groups), out_shape=[vme...]
where the time goes in v5:
time: 59.8 us; the launch traced here: 59.7 us
  Pallas kernels  59 us (99%)
  between operations  0.64 us (1%)
    pallas_call x1, Pallas kernels, fused(): pl.pallas_call(functools.partial(fused_kernel, n, groups), out_shape=[vme...  58.4 us

profile of v5, /device:TPU:0, one launch (start us, length us, event | category | flops | bytes accessed | tf_op | source)
XLA Modules:
  0.0 59.7 jit_solution(12899328035772444768)
XLA Ops:
  0.6 58.4 %experts.1 = (bf16[16,1024]{1,0:T(8,128)(2,1)S(1)}, bf16[16,1024]{1,0:T(8,128)(2,1)S(1)}) custom-call(bf16[16,1024]{1,0:T(8,128)(2,1)} %tok_hbm.1, bf16[16,1024]{1,0:T(8,128)(2,1)} %up_hbm.1, s32[8,16]{1,0:T(8,128)} %bitcast.3, f32[8,16]{1,0:T(8,128)} %bitcast.4, s32[1,16]{1,0:T(1,128)} %bitcast.5, bf16[1,2048,768]{2,1,0:T(8,128)(2,1)} %wg_hbm.1, ...), custom_call_target="tpu_custom_call" | custom-call | tf_op jit(solution)/shard_map/experts/pallas_call | solution.py:527
  59.0 0.6 %results.1 = (bf16[16,1024]{1,0:T(8,128)(2,1)}, bf16[16,1024]{1,0:T(8,128)(2,1)}) custom-call(bf16[16,1024]{1,0:T(8,128)(2,1)S(1)} %get-tuple-element.4.a_ref, bf16[16,1024]{1,0:T(8,128)(2,1)S(1)} %get-tuple-element.5.b_ref), custom_call_target="tpu_custom_call" | custom-call | tf_op jit(solution)/shard_map/results/pallas_call | solution.py:604

commit v6 on v5

--- a/solution.py
+++ b/solution.py
@@ -134,18 +134,15 @@
     near = list(range(1, chips))
     outer = near[::-1]
 
+    across = 4 * z + 2 * (1 - y) + parity
     barrier = pltpu.get_barrier_semaphore()
-    for d in reversed(range(1, n)):
+    partners = [(4 * flip(z, dz) + 2 * y + parity, h) for dz in reversed(range(1, columns))]
+    partners += [(across, other), (across, h), (e, other), (sibling, h)]
+    for partner in partners:
         pl.semaphore_signal(
-            barrier, inc=1, device_id=(flip(e, d), h), device_id_type=pl.DeviceIdType.MESH
+            barrier, inc=1, device_id=partner, device_id_type=pl.DeviceIdType.MESH
         )
-    for pe in (e, 4 * z + 2 * (1 - y) + parity):
-        pl.semaphore_signal(
-            barrier, inc=1, device_id=(pe, other), device_id_type=pl.DeviceIdType.MESH
-        )
-    pl.semaphore_wait(barrier, n + 1)
-
-    across = 4 * z + 2 * (1 - y) + parity
+    pl.semaphore_wait(barrier, len(partners))
 
     def spread(g, dz):
         slot = tok_buf.at[h, g, flip(z, dz), y, parity]
@@ -469,8 +466,8 @@
     turn(8, 9)
     layer_a = products(0)
     forward(1, chips // 2, chips)
+    mix(0)
     turn(9, 12)
-    mix(0)
     layer_b = products(1)
     relay(0, 0, 3 * chips // 8)
     mix(1)

time: 59.8 us -> 58.7 us (0.982)
  Pallas kernels: 59 us -> 57.9 us
    pallas_call x1, Pallas kernels: 58.4 us -> 57.3 us  [fused(): pl.pallas_call(functools.partial(fused_kernel, n, groups), out_shape=[vme...]
where the time goes in v6:
time: 58.7 us; the launch traced here: 58.6 us
  Pallas kernels  57.9 us (99%)
  between operations  0.64 us (1%)
    pallas_call x1, Pallas kernels, fused(): pl.pallas_call(functools.partial(fused_kernel, n, groups), out_shape=[vme...  57.3 us

profile of v6, /device:TPU:0, one launch (start us, length us, event | category | flops | bytes accessed | tf_op | source)
XLA Modules:
  0.0 58.6 jit_solution(5799689632003203095)
XLA Ops:
  0.6 57.3 %experts.1 = (bf16[16,1024]{1,0:T(8,128)(2,1)S(1)}, bf16[16,1024]{1,0:T(8,128)(2,1)S(1)}) custom-call(bf16[16,1024]{1,0:T(8,128)(2,1)} %tok_hbm.1, bf16[16,1024]{1,0:T(8,128)(2,1)} %up_hbm.1, s32[8,16]{1,0:T(8,128)} %bitcast.3, f32[8,16]{1,0:T(8,128)} %bitcast.4, s32[1,16]{1,0:T(1,128)} %bitcast.5, bf16[1,2048,768]{2,1,0:T(8,128)(2,1)} %wg_hbm.1, ...), custom_call_target="tpu_custom_call" | custom-call | tf_op jit(solution)/shard_map/experts/pallas_call | solution.py:524
  57.9 0.6 %results.1 = (bf16[16,1024]{1,0:T(8,128)(2,1)}, bf16[16,1024]{1,0:T(8,128)(2,1)}) custom-call(bf16[16,1024]{1,0:T(8,128)(2,1)S(1)} %get-tuple-element.4.a_ref, bf16[16,1024]{1,0:T(8,128)(2,1)S(1)} %get-tuple-element.5.b_ref), custom_call_target="tpu_custom_call" | custom-call | tf_op jit(solution)/shard_map/results/pallas_call | solution.py:601

commit v7 on v6

--- a/solution.py
+++ b/solution.py
@@ -72,10 +72,10 @@
     up_ref, ids_ref, probs_ref, pad_ref,
     tok_buf, wg, wu, wd, gate_v, up_v, act_v, hid, gg, gu,
     wg_t, wu_t, wd_t,
-    osend, orecv, ored, xrecv, xs, gram_s, share_s, gsend, grows, psend, prec,
+    osend, orecv, ored, xrecv, xs, gram_s, share_s, layer_s, gsend, grows, psend, prec,
     lsend, lrecv, lsum, lfin, rsend, rrecv, rsum, rfin,
     w_sem, line_ss, quad_ss, twin_ss, line_rs, quad_rs, twin_rs, part_ss, part_rs, out_ss, out_rs,
-    gram_ss, gram_rs, grad_ss, grad_rs, relay_ss, relay_rs, pair_ss, pair_rs, lpart_ss, lpart_rs, rpart_ss, rpart_rs, fin_ss, fin_rs,
+    gram_ss, gram_rs, grad_ss, grad_rs, relay_ss, relay_rs, pair_ss, pair_rs, lpart_ss, rpart_ss, fin_ss,
 ):
     e = lax.axis_index("expert")
     h = lax.axis_index("half")
@@ -265,20 +265,22 @@
     def share_of(g, pm):
         return share_s[g, pm][:, :, :1]
 
-    def products(g):
-        layer = jnp.zeros((sub, width), jnp.float32)
-        for d in [0] + near:
+    def taken(g, first, last):
+        part = jnp.zeros((sub, width), jnp.float32)
+        for d in range(first, last):
             pm = flip(chip, d)
             share = share_of(g, pm)
             arrived(xrecv.at[g, pm] if d else xrecv.at[g, chip, 1 - parity], out_rs.at[g, d])
             value = jnp.where(share > 0.0, xrecv[g, pm].astype(jnp.float32), 0.0)
             xs[g, pm] = value.astype(jnp.bfloat16)
-            layer = layer + jnp.sum(share * value, axis=0)
+            part = part + jnp.sum(share * value, axis=0)
+        layer_s[g] = layer_s[g] + part if first else part
+
+    def products(g):
         x_all = xs[g].reshape(rows, width)
         gram = dot_t(x_all, x_all).reshape(n, sub, rows) * same[None]
         gram_s[g, h] = jnp.sum(gram, axis=1)
         send(gram_s.at[g, h], gram_s.at[g, h], gram_ss, gram_rs.at[g], e, other)
-        return layer
 
     def mix(g):
         arrived(gram_s.at[g, other], gram_rs.at[g])
@@ -337,57 +339,58 @@
             else:
                 wu_t[:, at] = wu[at, :].T
 
+    left, right = slice(0, half_width), slice(half_width, width)
+
     def back(g, far):
         rows_at = pl.ds(g * rows, rows)
-        at = pl.ds(pl.multiple_of((other if far else h) * width, width), width)
-        part = dot(gg[rows_at, :], wg_t[:, at]) + dot(gu[rows_at, :], wu_t[:, at])
-        part = part.astype(jnp.bfloat16).reshape(columns, 2, 2, sub, width)
-        for q in range(2):
-            psend[g, far, q] = part[:, :, q]
-        send(
-            psend.at[g, far, 1 - parity], prec.at[g, far],
-            pair_ss, pair_rs.at[g, far], sibling, h,
-        )
-
-    left, right = slice(0, half_width), slice(half_width, width)
+        start = (other if far else h) * width
+        for k, cols in ((0, left), (1, right)) if far else ((1, right), (0, left)):
+            at = pl.ds(pl.multiple_of(start + k * half_width, half_width), half_width)
+            part = dot(gg[rows_at, :], wg_t[:, at]) + dot(gu[rows_at, :], wu_t[:, at])
+            part = part.astype(jnp.bfloat16).reshape(columns, 2, 2, sub, half_width)
+            for q in range(2):
+                psend[g, far, k, q] = part[:, :, q]
+            send(
+                psend.at[g, far, k, 1 - parity], prec.at[g, far, k],
+                pair_ss, pair_rs.at[g, far, k], sibling, h,
+            )
 
     def pairs(g):
-        arrived(prec.at[g, 1], pair_rs.at[g, 1])
+        arrived(prec.at[g, 1, 0], pair_rs.at[g, 1, 0])
         for dz in reversed(range(columns)):
             zz = flip(z, dz)
             lsend[g, zz] = (
-                psend[g, 1, parity, zz, :, :, left].astype(jnp.float32)
-                + prec[g, 1, zz, :, :, left].astype(jnp.float32)
+                psend[g, 1, 0, parity, zz].astype(jnp.float32)
+                + prec[g, 1, 0, zz].astype(jnp.float32)
             ).astype(jnp.bfloat16)
-            send(lsend.at[g, zz], lrecv.at[g, zz], lpart_ss, lpart_rs.at[g, dz], e, other)
+            send(lsend.at[g, zz], lrecv.at[g, zz], lpart_ss, line_rs.at[g, dz], e, other)
         for far in (1, 0):
-            if not far:
-                arrived(prec.at[g, 0], pair_rs.at[g, 0])
+            arrived(prec.at[g, far, 1], pair_rs.at[g, far, 1])
             for k in (1, 0):
                 zs = blocks(k)
                 rsend[g, far, zs] = (
-                    psend[g, far, parity, zs, 1 - y, :, right].astype(jnp.float32)
-                    + prec[g, far, zs, 1 - y, :, right].astype(jnp.float32)
+                    psend[g, far, 1, parity, zs, 1 - y].astype(jnp.float32)
+                    + prec[g, far, 1, zs, 1 - y].astype(jnp.float32)
                 ).astype(jnp.bfloat16)
                 send(
                     rsend.at[g, far, zs], rrecv.at[g, far, zs],
-                    rpart_ss, rpart_rs.at[g, far, k], across, h,
+                    rpart_ss, quad_rs.at[g, far, k], across, h,
                 )
 
     def finish_left(g, dz):
         zz = flip(z, dz)
         total = (
-            psend[g, 0, parity, zz, :, :, left].astype(jnp.float32)
-            + prec[g, 0, zz, :, :, left].astype(jnp.float32)
+            psend[g, 0, 0, parity, zz].astype(jnp.float32)
+            + prec[g, 0, 0, zz].astype(jnp.float32)
         )
-        arrived(lrecv.at[g, zz], lpart_rs.at[g, dz])
+        arrived(lrecv.at[g, zz], line_rs.at[g, dz])
         lsum[g, zz] = (total + lrecv[g, zz].astype(jnp.float32)).astype(jnp.bfloat16)
         for dy in (1, 0):
             yy = flip(y, dy)
             if dz or dy:
                 send(
                     lsum.at[g, zz, yy], lfin.at[g, chip],
-                    fin_ss.at[0], fin_rs.at[g, 0], 4 * zz + 2 * yy + parity, h,
+                    fin_ss.at[0], quad_rs.at[g, 2, 0], 4 * zz + 2 * yy + parity, h,
                 )
             else:
                 lfin[g, chip] = lsum[g, z, y]
@@ -395,22 +398,23 @@
     def finish_right(g, far, k):
         zs = blocks(k)
         total = (
-            psend[g, far, parity, zs, y, :, right].astype(jnp.float32)
-            + prec[g, far, zs, y, :, right].astype(jnp.float32)
+            psend[g, far, 1, parity, zs, y].astype(jnp.float32)
+            + prec[g, far, 1, zs, y].astype(jnp.float32)
         )
-        arrived(rrecv.at[g, far, zs], rpart_rs.at[g, far, k])
+        arrived(rrecv.at[g, far, zs], quad_rs.at[g, far, k])
         rsum[g, far, zs] = (total + rrecv[g, far, zs].astype(jnp.float32)).astype(jnp.bfloat16)
         for dz in reversed(range(k * block, (k + 1) * block)):
             zz = flip(z, dz)
             if dz or far:
                 send(
                     rsum.at[g, far, zz], rfin.at[g, columns * h + z],
-                    fin_ss.at[1], fin_rs.at[g, 1], 4 * zz + 2 * y + parity, other if far else h,
+                    fin_ss.at[1], quad_rs.at[g, 2, 1], 4 * zz + 2 * y + parity, other if far else h,
                 )
             else:
                 rfin[g, columns * h + z] = rsum[g, far, z]
 
     def finish(g):
+        arrived(prec.at[g, 0, 0], pair_rs.at[g, 0, 0])
         for k in (1, 0):
             for far in (1, 0):
                 for dz in reversed(range((2 * k + far) * block // 2, (2 * k + far + 1) * block // 2)):
@@ -418,8 +422,8 @@
                 finish_right(g, far, k)
 
     def collect(g):
-        arrived(lfin.at[g, pl.ds(0, chips - 1)], fin_rs.at[g, 0])
-        arrived(rfin.at[g, pl.ds(0, chips - 1)], fin_rs.at[g, 1])
+        arrived(lfin.at[g, pl.ds(0, chips - 1)], quad_rs.at[g, 2, 0])
+        arrived(rfin.at[g, pl.ds(0, chips - 1)], quad_rs.at[g, 2, 1])
         return [jnp.sum(fin[g].astype(jnp.float32), axis=0) for fin in (lfin, rfin)]
 
     lines(0)
@@ -462,16 +466,19 @@
     turn(6, 7)
     forward(1, chips // 4, 3 * chips // 8)
     turn(7, 8)
+    taken(0, 0, chips // 2)
     forward(1, 3 * chips // 8, chips // 2)
     turn(8, 9)
-    layer_a = products(0)
+    taken(0, chips // 2, chips)
+    products(0)
     forward(1, chips // 2, chips)
     mix(0)
     turn(9, 12)
-    layer_b = products(1)
+    taken(1, 0, chips)
+    products(1)
     relay(0, 0, 3 * chips // 8)
     mix(1)
-    layer_ref[...] = jnp.concatenate([layer_a, layer_b], axis=0).astype(jnp.bfloat16)
+    layer_ref[...] = layer_s[...].reshape(tok, width).astype(jnp.bfloat16)
     relay(0, 3 * chips // 8, chips)
     relay(1, 0, 5 * chips // 8)
     act(0, 0)
@@ -503,7 +510,7 @@
     drained(gsend.at[:, pl.ds(0, chips - 1)], grad_ss.at[0])
     drained(gsend.at[:, 0, 0], grad_ss.at[1])
     drained(grows.at[0], relay_ss)
-    drained(psend.at[:, :, 0], pair_ss)
+    drained(psend.at[:, :, :, 0], pair_ss)
     drained(lsend, lpart_ss)
     drained(rsend, rpart_ss)
     drained(lfin.at[:, pl.ds(0, chips - 1)], fin_ss.at[0])
@@ -551,10 +558,11 @@
             vmem((groups, chips, 2, sub, width), low),
             vmem((groups, 2, n, n * sub), wide),
             vmem((groups, chips, 2, sub, 128), wide),
+            vmem((groups, sub, width), wide),
             vmem((groups, chips, 2, sub, width), low),
             vmem((2, groups, chips, 2, sub, width), low),
-            vmem((groups, 2, 2, columns, 2, sub, width), low),
-            vmem((groups, 2, columns, 2, sub, width), low),
+            vmem((groups, 2, 2, 2, columns, 2, sub, width // 2), low),
+            vmem((groups, 2, 2, columns, 2, sub, width // 2), low),
             vmem((groups, columns, 2, sub, width // 2), low),
             vmem((groups, columns, 2, sub, width // 2), low),
             vmem((groups, columns, 2, sub, width // 2), low),
@@ -581,13 +589,10 @@
             dma(()),
             dma((groups,)),
             dma(()),
-            dma((groups, 2)),
-            dma(()),
-            dma((groups, columns)),
-            dma(()),
             dma((groups, 2, 2)),
+            dma(()),
+            dma(()),
             dma((2,)),
-            dma((groups, 2)),
         ],
         compiler_params=pltpu.CompilerParams(
             collective_id=0, has_side_effects=True, vmem_limit_bytes=56 * 1024 * 1024

time: 58.7 us -> 58.7 us (level)
  no operation moved by 1% of the time
where the time goes in v7:
time: 58.7 us; the launch traced here: 58.5 us
  Pallas kernels  57.9 us (99%)
  between operations  0.64 us (1%)
    pallas_call x1, Pallas kernels, fused(): pl.pallas_call(functools.partial(fused_kernel, n, groups), out_shape=[vme...  57.3 us

profile of v7, /device:TPU:0, one launch (start us, length us, event | category | flops | bytes accessed | tf_op | source)
XLA Modules:
  0.0 58.5 jit_solution(6889017137302050267)
XLA Ops:
  0.6 57.3 %experts.1 = (bf16[16,1024]{1,0:T(8,128)(2,1)S(1)}, bf16[16,1024]{1,0:T(8,128)(2,1)S(1)}) custom-call(bf16[16,1024]{1,0:T(8,128)(2,1)} %tok_hbm.1, bf16[16,1024]{1,0:T(8,128)(2,1)} %up_hbm.1, s32[8,16]{1,0:T(8,128)} %bitcast.3, f32[8,16]{1,0:T(8,128)} %bitcast.4, s32[1,16]{1,0:T(1,128)} %bitcast.5, bf16[1,2048,768]{2,1,0:T(8,128)(2,1)} %wg_hbm.1, ...), custom_call_target="tpu_custom_call" | custom-call | tf_op jit(solution)/shard_map/experts/pallas_call | solution.py:531
  57.9 0.6 %results.1 = (bf16[16,1024]{1,0:T(8,128)(2,1)}, bf16[16,1024]{1,0:T(8,128)(2,1)}) custom-call(bf16[16,1024]{1,0:T(8,128)(2,1)S(1)} %get-tuple-element.4.a_ref, bf16[16,1024]{1,0:T(8,128)(2,1)S(1)} %get-tuple-element.5.b_ref), custom_call_target="tpu_custom_call" | custom-call | tf_op jit(solution)/shard_map/results/pallas_call | solution.py:606

commit v8 on v7

--- a/solution.py
+++ b/solution.py
@@ -72,7 +72,7 @@
     up_ref, ids_ref, probs_ref, pad_ref,
     tok_buf, wg, wu, wd, gate_v, up_v, act_v, hid, gg, gu,
     wg_t, wu_t, wd_t,
-    osend, orecv, ored, xrecv, xs, gram_s, share_s, layer_s, gsend, grows, psend, prec,
+    osend, orecv, ored, xrecv, xmore, xs, gram_s, share_s, layer_s, gsend, grows, psend, prec,
     lsend, lrecv, lsum, lfin, rsend, rrecv, rsum, rfin,
     w_sem, line_ss, quad_ss, twin_ss, line_rs, quad_rs, twin_rs, part_ss, part_rs, out_ss, out_rs,
     gram_ss, gram_rs, grad_ss, grad_rs, relay_ss, relay_rs, pair_ss, pair_rs, lpart_ss, rpart_ss, fin_ss,
@@ -234,13 +234,33 @@
 
         tiles(width, down_step, 1024)
 
+    def straight(g, d):
+        return g == 0 and d == chips - 1
+
     def cross_parts(g):
         for d in outer + [0]:
             pm = flip(chip, d)
-            send(osend.at[g, 1, pm], orecv.at[g, pm], part_ss, part_rs.at[g, d], e, other)
+            if straight(g, d):
+                for q in range(2):
+                    send(
+                        osend.at[g, 1, pm, q], xmore.at[parity],
+                        part_ss, out_rs.at[g, d], 2 * pm + q, other,
+                    )
+            else:
+                send(osend.at[g, 1, pm], orecv.at[g, pm], part_ss, part_rs.at[g, d], e, other)
+
+    def own_parts(g):
+        pm = flip(chip, chips - 1)
+        for q in range(2):
+            send(
+                osend.at[g, 0, pm, q], xrecv.at[g, chip, parity],
+                out_ss.at[0], out_rs.at[g, chips - 1], 2 * pm + q, h,
+            )
 
     def forward(g, first, last):
         for d in (outer + [0])[first:last]:
+            if straight(g, d):
+                continue
             pm = flip(chip, d)
             arrived(orecv.at[g, pm], part_rs.at[g, d])
             total = osend[g, 0, pm].astype(jnp.float32) + orecv[g, pm].astype(jnp.float32)
@@ -270,8 +290,12 @@
         for d in range(first, last):
             pm = flip(chip, d)
             share = share_of(g, pm)
-            arrived(xrecv.at[g, pm] if d else xrecv.at[g, chip, 1 - parity], out_rs.at[g, d])
-            value = jnp.where(share > 0.0, xrecv[g, pm].astype(jnp.float32), 0.0)
+            result = xrecv.at[g, pl.ds(0, 2)] if straight(g, d) else xrecv.at[g, pm]
+            arrived(result if d else xrecv.at[g, chip, 1 - parity], out_rs.at[g, d])
+            value = xrecv[g, pm].astype(jnp.float32)
+            if straight(g, d):
+                value = (value + xmore[...].astype(jnp.float32)).astype(jnp.bfloat16).astype(jnp.float32)
+            value = jnp.where(share > 0.0, value, 0.0)
             xs[g, pm] = value.astype(jnp.bfloat16)
             part = part + jnp.sum(share * value, axis=0)
         layer_s[g] = layer_s[g] + part if first else part
@@ -355,7 +379,7 @@
                 pair_ss, pair_rs.at[g, far, k], sibling, h,
             )
 
-    def pairs(g):
+    def pairs_left(g):
         arrived(prec.at[g, 1, 0], pair_rs.at[g, 1, 0])
         for dz in reversed(range(columns)):
             zz = flip(z, dz)
@@ -364,6 +388,8 @@
                 + prec[g, 1, 0, zz].astype(jnp.float32)
             ).astype(jnp.bfloat16)
             send(lsend.at[g, zz], lrecv.at[g, zz], lpart_ss, line_rs.at[g, dz], e, other)
+
+    def pairs_right(g):
         for far in (1, 0):
             arrived(prec.at[g, far, 1], pair_rs.at[g, far, 1])
             for k in (1, 0):
@@ -438,8 +464,9 @@
     loads[-1].wait()
     down(0, 1)
     cross_parts(0)
+    down(0, 0)
+    own_parts(0)
     gathered(1)
-    down(0, 0)
     twins(1, h)
     own_rows(1)
     twins(1, other)
@@ -463,15 +490,17 @@
     forward(1, 0, chips // 8)
     turn(5, 6)
     forward(1, chips // 8, chips // 4)
-    turn(6, 7)
+    taken(0, 0, chips // 2)
     forward(1, chips // 4, 3 * chips // 8)
-    turn(7, 8)
-    taken(0, 0, chips // 2)
-    forward(1, 3 * chips // 8, chips // 2)
-    turn(8, 9)
     taken(0, chips // 2, chips)
     products(0)
-    forward(1, chips // 2, chips)
+    forward(1, 3 * chips // 8, 5 * chips // 8)
+    turn(6, 7)
+    forward(1, 5 * chips // 8, 3 * chips // 4)
+    turn(7, 8)
+    forward(1, 3 * chips // 4, 7 * chips // 8)
+    turn(8, 9)
+    forward(1, 7 * chips // 8, chips)
     mix(0)
     turn(9, 12)
     taken(1, 0, chips)
@@ -488,12 +517,14 @@
     back(0, 1)
     back(0, 0)
     act(1, 0)
-    pairs(0)
+    pairs_left(0)
+    pairs_right(0)
     act(1, 1)
     back(1, 1)
     back(1, 0)
+    pairs_left(1)
     finish(0)
-    pairs(1)
+    pairs_right(1)
     finish(1)
     total_a = collect(0)
     total_b = collect(1)
@@ -555,6 +586,7 @@
             vmem((groups, chips, 2, sub, width), low),
             vmem((groups, chips, 2, sub, width), low),
             vmem((groups, chips, 2, sub, width), low),
+            vmem((2, sub, width), low),
             vmem((groups, chips, 2, sub, width), low),
             vmem((groups, 2, n, n * sub), wide),
             vmem((groups, chips, 2, sub, 128), wide),

time: 58.7 us -> 58.7 us (level)
  no operation moved by 1% of the time
where the time goes in v8:
time: 58.7 us; the launch traced here: 58.5 us
  Pallas kernels  57.9 us (99%)
  between operations  0.64 us (1%)
    pallas_call x1, Pallas kernels, fused(): pl.pallas_call(functools.partial(fused_kernel, n, groups), out_shape=[vme...  57.3 us

profile of v8, /device:TPU:0, one launch (start us, length us, event | category | flops | bytes accessed | tf_op | source)
XLA Modules:
  0.0 58.5 jit_solution(14551556483190525087)
XLA Ops:
  0.6 57.3 %experts.1 = (bf16[16,1024]{1,0:T(8,128)(2,1)S(1)}, bf16[16,1024]{1,0:T(8,128)(2,1)S(1)}) custom-call(bf16[16,1024]{1,0:T(8,128)(2,1)} %tok_hbm.1, bf16[16,1024]{1,0:T(8,128)(2,1)} %up_hbm.1, s32[8,16]{1,0:T(8,128)} %bitcast.3, f32[8,16]{1,0:T(8,128)} %bitcast.4, s32[1,16]{1,0:T(1,128)} %bitcast.5, bf16[1,2048,768]{2,1,0:T(8,128)(2,1)} %wg_hbm.1, ...), custom_call_target="tpu_custom_call" | custom-call | tf_op jit(solution)/shard_map/experts/pallas_call | solution.py:562
  57.9 0.6 %results.1 = (bf16[16,1024]{1,0:T(8,128)(2,1)}, bf16[16,1024]{1,0:T(8,128)(2,1)}) custom-call(bf16[16,1024]{1,0:T(8,128)(2,1)S(1)} %get-tuple-element.4.a_ref, bf16[16,1024]{1,0:T(8,128)(2,1)S(1)} %get-tuple-element.5.b_ref), custom_call_target="tpu_custom_call" | custom-call | tf_op jit(solution)/shard_map/results/pallas_call | solution.py:638
